TPU v7x, 32 devices: a whole 2x2x4 slice. The times are simulated.
32 devices in a mesh: dp: 4 (over z), row: 4 (over x, core), col: 2 (over y).
Axes of the slice: x: 2, y: 2, z: 4, core: 2. Of those that a mesh axis runs over, the one named last changes fastest.
Arguments:
- tokens: bfloat16 [11664, 1152], P(('dp', 'col'), 'row'), may hold values from -6 to 6
- ln_gain: bfloat16 [2, 1152], P(None, 'row'), may hold values from 0.5 to 1.5
- ln_bias: bfloat16 [2, 1152], P(None, 'row'), may hold values from -3 to 3
- w_qkv: bfloat16 [1152, 3, 1152], P('row', None, 'col'), may hold values from -0.1875 to 0.1875
- b_qv: bfloat16 [2, 1152], P(None, 'col'), may hold values from -3 to 3
- w_out: bfloat16 [1152, 1152], P('col', 'row'), may hold values from -3 to 3
- b_out: bfloat16 [1152], P('row'), may hold values from -3 to 3
- w_up: bfloat16 [1152, 4304], P('row', 'col'), may hold values from -0.1875 to 0.1875
- b_up: bfloat16 [4304], P('col'), may hold values from -3 to 3
- w_down: bfloat16 [4304, 1152], P('col', 'row'), may hold values from -0.09375 to 0.09375
- b_down: bfloat16 [1152], P('row'), may hold values from -3 to 3
- cotangent: bfloat16 [11664, 1152], P(('dp', 'col'), 'row'), may hold values from -6 to 6
Outputs:
- output: bfloat16 [11664, 1152], P(('dp', 'col'), 'row')
- input_grad: bfloat16 [11664, 1152], P(('dp', 'col'), 'row')
- d_ln_gain: float32 [2, 1152], P(None, 'row')
- d_ln_bias: float32 [2, 1152], P(None, 'row')
- d_w_qkv: float32 [1152, 3, 1152], P(('row', 'dp'), None, 'col')
- d_b_qv: float32 [2, 1152], P(None, 'col')
- d_w_out: float32 [1152, 1152], P(('col', 'dp'), 'row')
- d_b_out: float32 [1152], P('row')
- d_w_up: float32 [1152, 4304], P(('row', 'dp'), 'col')
- d_b_up: float32 [4304], P('col')
- d_w_down: float32 [4304, 1152], P('col', ('row', 'dp'))
- d_b_down: float32 [1152], P('row')
All inputs are finite; a program needn't handle non-finite values.
Results may differ from a plain program's by a relative error of at most 0.018.
Values may be sent and summed in bfloat16 or wider, within the bound.
A program may use at most 192 MiB of HBM per device.

v0:
```python
import jax
import jax.numpy as jnp
from jax import lax
from jax.experimental import pallas as pl
from jax.experimental.pallas import tpu as pltpu
from jax.sharding import PartitionSpec as P

HD = 72
SEQ = 729
EPS = 1e-06
BF = jnp.bfloat16
F32 = jnp.float32


def nn(a, b):
    return jnp.dot(a, b, preferred_element_type=F32)


def nt(a, b):
    return lax.dot_general(a, b, (((1,), (1,)), ((), ())), preferred_element_type=F32)


def tn(a, b):
    return lax.dot_general(a, b, (((0,), (0,)), ((), ())), preferred_element_type=F32)


def gelu_parts(u):
    t = jnp.tanh(0.7978845608028654 * (u + 0.044715 * u * u * u))
    value = 0.5 * u * (1.0 + t)
    slope = 0.5 * (1.0 + t) + 0.5 * u * (1.0 - t * t) * 0.7978845608028654 * (1.0 + 3 * 0.044715 * u * u)
    return value, slope


MESH = pl.DeviceIdType.MESH
PADS = 736
VMEM_CAP = 66_000_000


def place():
    row, col = lax.axis_index("row"), lax.axis_index("col")
    return row // 2, lax.rem(row, 2), col


def at(x, k, y):
    return {"row": 2 * x + k, "col": y}


def greet(peers):
    barrier = pltpu.get_barrier_semaphore()
    for peer in peers:
        pl.semaphore_signal(barrier, inc=1, device_id=peer, device_id_type=MESH)
    pl.semaphore_wait(barrier, len(peers))


def chunks(total, step, body):
    whole = total // step
    if whole > 0:
        lax.fori_loop(0, whole, lambda i, c: (body(pl.multiple_of(i * step, step), step), c)[1], 0)
    if total % step:
        body(whole * step, total % step)


def column(part, head, hw):
    half, left = divmod(head, hw // HD // 2)
    return half * (padded(hw) // 2) + part * (hw // 2) + left * HD


def padded(hw):
    return 2 * (-(-3 * hw // 2 // 128) * 128)


class Moves:
    def __init__(self, sems):
        self.sems, self.open = sems, {}

    def start(self, src, dst):
        c = pltpu.make_async_copy(src, dst, self.sems.at[len(self.open)])
        c.start()
        self.open[len(self.open)] = c
        return c

    def finish(self):
        for c in self.open.values():
            c.wait()


def forward_kernel(
    tok, cot, bias, wq, wo, wu, wd,
    gq, go, gu, gd, xb_h, dyb_h, f1b_h, qh_h, oh_h, hflat_h, lse_h, residual_h, f2b_h, hidden_h, slope_h, dd_h,
    xb, dyb, bv, f1b, qh, oh, hflat, lse, residual, f2b, hidden, slope, dd,
    tbuf, cbuf, gqv, gov, guv, f1, psend, precv,
    ssem, rsem, csem, lsem, wsend, wrecv, msem,
):
    x, k, y = place()
    is_a, is_b = k == y, k != y
    hw = hflat.shape[1]
    heads = hw // HD
    width = tok.shape[2]
    greet([at(x, 1 - k, y), at(1 - x, k, y), at(1 - x, 1 - k, y), at(x, k, 1 - y), at(x, 1 - k, 1 - y)])

    def remote(src, dst, s, r, dest):
        return pltpu.make_async_remote_copy(
            src_ref=src, dst_ref=dst, send_sem=s, recv_sem=r, device_id=dest, device_id_type=MESH
        )

    blocks, wholes = (wq, wo, wu, wd), (gq, go, gu, gd)
    out = Moves(msem)

    def own_sends(w):
        b, g = blocks[w], wholes[w]
        a = [
            remote(b, g.at[2 + k], wsend.at[w, 0], wrecv.at[w, 2 + k], at(1 - x, k, y)),
            remote(b, g.at[k], wsend.at[w, 1], wrecv.at[w, k], at(x, k, 1 - y)),
        ]
        bb = [
            remote(b, g.at[2 + k], wsend.at[w, 0], wrecv.at[w, 2 + k], at(1 - x, 1 - k, y)),
            remote(b, g.at[k], wsend.at[w, 1], wrecv.at[w, k], at(x, 1 - k, 1 - y)),
            remote(b, g.at[k], wsend.at[w, 2], wrecv.at[w, k], at(x, 1 - k, y)),
        ]
        return a, bb

    def relays(w):
        g = wholes[w]
        return (
            remote(g.at[2], g.at[2], wsend.at[w, 3], wrecv.at[w, 2], at(x, k, 1 - y)),
            remote(g.at[1], g.at[3], wsend.at[w, 3], wrecv.at[w, 3], at(1 - x, k, y)),
        )

    def both(fa, fb):
        pl.when(is_a)(fa)
        pl.when(is_b)(fb)

    def start_own(w):
        a, b = own_sends(w)
        both(lambda: [c.start() for c in a] and None, lambda: [c.start() for c in b] and None)

    def arrived(w, j):
        remote(blocks[w], wholes[w].at[j], wsend.at[w, 0], wrecv.at[w, j], at(x, 1 - k, y)).wait_recv()

    def start_relay(w):
        ra, rb = relays(w)

        def fa():
            arrived(w, 2)
            ra.start()

        def fb():
            arrived(w, 1)
            rb.start()

        both(fa, fb)

    def wait_rest(w):
        pl.when(is_b | (k == 1))(lambda: arrived(w, 0))
        pl.when(is_a & (k == 0))(lambda: arrived(w, 1))
        pl.when(is_b)(lambda: arrived(w, 2))
        arrived(w, 3)

    def finish_sends(w):
        a, b = own_sends(w)
        ra, rb = relays(w)
        both(
            lambda: [c.wait_send() for c in a + [ra]] and None,
            lambda: [c.wait_send() for c in b + [rb]] and None,
        )

    def load(w, dst):
        b, g = blocks[w], wholes[w]
        for j in range(4):
            rows = pl.ds(j * width, width)
            local = is_a & (k == j) if j < 2 else None
            if local is None:
                pltpu.make_async_copy(g.at[j], dst.at[rows], lsem.at[j]).start()
            else:
                pl.when(local)(lambda: pltpu.make_async_copy(b, dst.at[rows], lsem.at[j]).start())
                pl.when(jnp.logical_not(local))(
                    lambda: pltpu.make_async_copy(g.at[j], dst.at[rows], lsem.at[j]).start()
                )
        for j in range(4):
            pltpu.make_async_copy(g.at[j], dst.at[pl.ds(j * width, width)], lsem.at[j]).wait()

    tx = remote(tok.at[1 - x], tbuf.at[2 + k], ssem.at[0], rsem.at[0], at(1 - x, k, y))
    cx = remote(cot.at[1 - x], cbuf.at[2 + k], ssem.at[1], rsem.at[1], at(1 - x, k, y))
    t1 = remote(tok.at[x], tbuf.at[k], ssem.at[2], rsem.at[2], at(x, 1 - k, y))
    c1 = remote(cot.at[x], cbuf.at[k], ssem.at[3], rsem.at[3], at(x, 1 - k, y))
    t2 = remote(tbuf.at[2 + k], tbuf.at[2 + k], ssem.at[4], rsem.at[4], at(x, 1 - k, y))
    c2 = remote(cbuf.at[2 + k], cbuf.at[2 + k], ssem.at[5], rsem.at[5], at(x, 1 - k, y))
    bs = remote(bias, bv, ssem.at[6], rsem.at[6], at(x, k, 1 - y))
    pe = remote(psend, precv, ssem.at[7], rsem.at[7], at(x, 1 - k, y))
    tl = pltpu.make_async_copy(tok.at[x], tbuf.at[k], csem.at[0])
    cl = pltpu.make_async_copy(cot.at[x], cbuf.at[k], csem.at[1])
    bl = pltpu.make_async_copy(bias, bv, csem.at[2])

    tx.start()
    t1.start()
    tl.start()
    start_own(0)
    both(lambda: (bl.start(), bs.start()) and None, lambda: None)
    cl.start()
    c1.start()

    tx.wait_recv()
    t2.start()
    tl.wait()
    t1.wait_recv()
    t2.wait_recv()
    for j in range(4):
        xb[:, j * width : (j + 1) * width] = tbuf[j]
    vecs = xb[SEQ - 1 : PADS, :].astype(F32)
    g1, g2, s1, s2, bo = (vecs[j : j + 1] for j in range(1, 6))

    def stats(v):
        mean = jnp.mean(v, axis=1, keepdims=True)
        c = v - mean
        return c * lax.rsqrt(jnp.mean(c * c, axis=1, keepdims=True) + EPS)

    def norm1(r, n):
        f1[pl.ds(r, n), :] = (stats(xb[pl.ds(r, n), :].astype(F32)) * g1 + s1).astype(BF)

    chunks(PADS, 128, norm1)
    f2 = f1
    start_relay(0)
    start_own(1)
    both(bl.wait, bs.wait_recv)
    wait_rest(0)
    load(0, gqv)

    def project(c, n):
        cols = pl.ds(c, n)
        hidden[:, cols] = (nn(f1[...], gqv[:, cols]) + bv[0:1, cols].astype(F32)).astype(BF)

    chunks(gqv.shape[1], 256, project)
    start_relay(1)
    start_own(2)
    for j in range(4):
        f1b[j] = f1[:, j * width : (j + 1) * width]
    qh[...] = jnp.zeros_like(qh)
    for p in range(3):
        for h in range(heads):
            lo = column(p, h, hw)
            qh[p * heads + h, :, 0:HD] = hidden[:, lo : lo + HD]
    out.start(xb, xb_h)
    out.start(f1b, f1b_h)
    out.start(qh, qh_h)
    keymask = jnp.where(lax.broadcasted_iota(jnp.int32, (PADS, 1), 0) < SEQ, 0.0, -1e30)

    def attend(h, carry):
        st = nt(qh[heads + h], qh[h]) + keymask
        top = jnp.max(st, axis=0, keepdims=True)
        e = jnp.exp((st - top) * HD ** (-0.5))
        tot = jnp.sum(e, axis=0, keepdims=True)
        lse[pl.ds(h, 1), :] = top * HD ** (-0.5) + jnp.log(tot)
        out = tn(qh[2 * heads + h], e.astype(BF)) / tot
        oh[h] = out.T.astype(BF)
        return carry

    lax.fori_loop(0, heads, attend, 0)
    for h in range(heads):
        hflat[:, h * HD : (h + 1) * HD] = oh[h, :, 0:HD]
    out.start(oh, oh_h)
    out.start(hflat, hflat_h)
    out.start(lse, lse_h)
    wait_rest(1)
    load(1, gov)

    def out_project(c, n):
        cols = pl.ds(c, n)
        part = nt(hflat[...], gov[cols, :])
        psend[:, cols] = part.astype(BF)
        residual[:, cols] = part

    chunks(4 * width, 384, out_project)
    pe.start()
    pe.wait_recv()

    def norm2(r, n):
        rows = pl.ds(r, n)
        v = xb[rows, :].astype(F32) + bo + residual[rows, :] + precv[rows, :].astype(F32)
        residual[rows, :] = v
        f2[rows, :] = (stats(v) * g2 + s2).astype(BF)

    chunks(PADS, 128, norm2)
    start_relay(2)
    cx.start()
    start_own(3)
    wait_rest(2)
    load(2, guv)
    for j in range(4):
        f2b[j] = f2[:, j * width : (j + 1) * width]
    out.start(residual, residual_h)
    out.start(f2b, f2b_h)

    def expand(c, n):
        cols = pl.ds(c, n)
        u = nn(f2[...], guv[:, cols]) + bv[1:2, cols].astype(F32)
        value, grad = gelu_parts(u)
        hidden[:, cols] = value.astype(BF)
        slope[:, cols] = grad.astype(BF)

    chunks(hidden.shape[1], 256, expand)
    out.start(hidden, hidden_h)
    out.start(slope, slope_h)
    cx.wait_recv()
    c2.start()
    cl.wait()
    c1.wait_recv()
    c2.wait_recv()
    for j in range(4):
        dyb[:, j * width : (j + 1) * width] = cbuf[j]

    def down_grad(j, carry):
        dd[j] = tn(cbuf[j], hidden[...]).astype(BF)
        return carry

    out.start(dyb, dyb_h)
    lax.fori_loop(0, 4, down_grad, 0)
    out.start(dd, dd_h)
    start_relay(3)
    wait_rest(3)
    for c in (tx, cx, t1, c1, t2, c2, pe):
        c.wait_send()
    both(bs.wait_send, lambda: None)
    for w in range(4):
        finish_sends(w)
    out.finish()


def forward(tok, cot, bias, wq, wo, wu, wd):
    width, hw, ff = tok.shape[2], wo.shape[1], wu.shape[1]
    full = 4 * width
    heads = hw // HD
    anyspec = pl.BlockSpec(memory_space=pl.ANY)
    shape = jax.ShapeDtypeStruct
    outs = [
        shape((4,) + wq.shape, BF), shape((4,) + wo.shape, BF), shape((4,) + wu.shape, BF), shape((4,) + wd.shape, BF),
        shape((PADS, full), BF), shape((PADS, full), BF), shape((4, PADS, width), BF),
        shape((3 * heads, PADS, 128), BF), shape((heads, PADS, 128), BF), shape((PADS, hw), BF), shape((heads, PADS), F32),
        shape((PADS, full), F32), shape((4, PADS, width), BF), shape((PADS, ff), BF), shape((PADS, ff), BF),
        shape((4, width, ff), BF),
    ]
    dma = pltpu.SemaphoreType.DMA
    return pl.pallas_call(
        forward_kernel,
        out_shape=outs,
        in_specs=[anyspec] * 7,
        out_specs=[anyspec] * len(outs),
        scratch_shapes=[pltpu.VMEM(o.shape, o.dtype) for o in outs[4:6]] + [pltpu.VMEM(bias.shape, BF)]
        + [pltpu.VMEM(o.shape, o.dtype) for o in outs[6:]]
        + [
            pltpu.VMEM((4, PADS, width), BF), pltpu.VMEM((4, PADS, width), BF),
            pltpu.VMEM((full, wq.shape[1]), BF), pltpu.VMEM((full, hw), BF), pltpu.VMEM((full, ff), BF),
            pltpu.VMEM((PADS, full), BF), pltpu.VMEM((PADS, full), BF), pltpu.VMEM((PADS, full), BF),
            dma((8,)), dma((8,)), dma((3,)), dma((4,)), dma((4, 4)), dma((4, 4)), dma((12,)),
        ],
        compiler_params=pltpu.CompilerParams(collective_id=0, has_side_effects=True, vmem_limit_bytes=VMEM_CAP),
        name="forward",
    )(tok, cot, bias, wq, wo, wu, wd)


def load_weight(b, g, dst, sem, k, is_a):
    width = b.shape[0]
    for j in range(4):
        rows = pl.ds(j * width, width)
        if j < 2:
            local = is_a & (k == j)
            pl.when(local)(lambda: pltpu.make_async_copy(b, dst.at[rows], sem.at[j]).start())
            pl.when(jnp.logical_not(local))(lambda: pltpu.make_async_copy(g.at[j], dst.at[rows], sem.at[j]).start())
        else:
            pltpu.make_async_copy(g.at[j], dst.at[rows], sem.at[j]).start()

    def wait():
        for j in range(4):
            pltpu.make_async_copy(g.at[j], dst.at[pl.ds(j * width, width)], sem.at[j]).wait()

    return wait


def remote(src, dst, s, r, dest):
    return pltpu.make_async_remote_copy(
        src_ref=src, dst_ref=dst, send_sem=s, recv_sem=r, device_id=dest, device_id_type=MESH
    )


class Scatter:
    def __init__(self, d, r, zs, st, sb, cv, ss, rs, ls, spot):
        self.d, self.r, self.zs, self.st, self.sb, self.cv, self.ls, self.spot = d, r, zs, st, sb, cv, ls, spot
        x, k, y = spot
        self.is_a, self.is_b, self.k = k == y, k != y, k
        across, over, mate = at(1 - x, k, y), at(x, k, 1 - y), at(x, 1 - k, y)
        self.x1 = remote(d.at[2], r.at[0], ss.at[0], rs.at[0], across)
        self.y1 = remote(d.at[3], r.at[1], ss.at[1], rs.at[1], over)
        self.y1b = remote(d.at[1], r.at[2], ss.at[2], rs.at[2], over)
        self.x2 = remote(sb, r.at[3], ss.at[1], rs.at[3], across)
        self.y2 = remote(sb, r.at[4], ss.at[3], rs.at[4], over)
        if zs is not None:
            self.home = remote(cv.at[1], zs, ss.at[2], rs.at[5], mate)

    def first(self):
        self.x1.start()

        def b():
            self.y1.start()
            self.y1b.start()

        pl.when(self.is_b)(b)

    def copy_in(self, pairs):
        for i, src in pairs:
            pltpu.make_async_copy(src, self.st.at[i], self.ls.at[i]).start()
        for i, src in pairs:
            pltpu.make_async_copy(src, self.st.at[i], self.ls.at[i]).wait()

    def second(self):
        st, sb = self.st, self.sb

        def fetch_a():
            self.y1.wait_recv()
            self.copy_in([(0, self.d.at[3]), (1, self.r.at[1])])

        def fetch_b():
            self.x1.wait_recv()
            self.copy_in([(0, self.d.at[0]), (1, self.r.at[0])])

        pl.when(self.is_a)(fetch_a)
        pl.when(self.is_b)(fetch_b)

        def add(c, n):
            cols = pl.ds(c, n)
            sb[:, cols] = (st[0, :, cols].astype(F32) + st[1, :, cols].astype(F32)).astype(BF)

        chunks(sb.shape[1], 128, add)
        pl.when(self.is_a)(self.x2.start)
        pl.when(self.is_b)(self.y2.start)

    def settle(self):
        def a():
            self.x1.wait_recv()
            self.y1b.wait_recv()
            self.x2.wait_recv()
            self.y2.wait_recv()

        pl.when(self.is_a)(a)

    def third(self, settled=False):
        if not settled:
            self.settle()
        st, cv = self.st, self.cv
        parts, piece = cv.shape[1], cv.shape[2]

        def a():
            d, r = self.d, self.r
            for which, trio in ((self.k, (d.at[0], r.at[0], r.at[4])), (1 - self.k, (d.at[1], r.at[2], r.at[3]))):
                self.copy_in(list(enumerate(trio)))

                def add(c, n):
                    cols = pl.ds(c, n)
                    total = sum(st[i, :, cols].astype(F32) for i in range(3))
                    for q in range(parts):
                        cv[which, q, :, cols] = total[q * piece : (q + 1) * piece].astype(BF)

                chunks(cv.shape[3], 128, add)
            self.home.start()
            keep = pltpu.make_async_copy(cv.at[0], self.zs, self.ls.at[0])
            keep.start()
            keep.wait()

        pl.when(self.is_a)(a)

    def fourth(self):
        pl.when(self.is_b)(self.home.wait_recv)

    def home_sent(self):
        pl.when(self.is_a)(self.home.wait_send)

    def close(self, home=True):
        self.x1.wait_send()
        pl.when(self.is_a)(self.x2.wait_send)
        if home:
            self.home_sent()

        def b():
            self.y1.wait_send()
            self.y1b.wait_send()
            self.y2.wait_send()

        pl.when(self.is_b)(b)

    @staticmethod
    def peers(spot):
        x, k, y = spot
        return [at(1 - x, k, y), at(x, k, 1 - y), at(x, 1 - k, y)]


def scatter_scratch(rows, cols, parts):
    return [
        pltpu.VMEM((3, rows, cols), BF), pltpu.VMEM((rows, cols), BF), pltpu.VMEM((2, parts, rows // parts, cols), BF),
        pltpu.SemaphoreType.DMA((4,)), pltpu.SemaphoreType.DMA((6,)), pltpu.SemaphoreType.DMA((6,)),
    ]


def norm_back_rows(values, mine, theirs, gain):
    mean = jnp.mean(values, axis=1, keepdims=True)
    center = values - mean
    scale = lax.rsqrt(jnp.mean(center * center, axis=1, keepdims=True) + EPS)
    normed = center * scale
    incoming = mine.astype(F32) + theirs.astype(F32)
    e = incoming * gain
    back = scale * (e - jnp.mean(e, axis=1, keepdims=True) - normed * jnp.mean(e * normed, axis=1, keepdims=True))
    return back, normed, incoming


def fold(acc, i, rows):
    acc[i] += sum(rows[8 * j : 8 * j + 8] for j in range(rows.shape[0] // 8))


def middle_kernel(
    dd, gd, wd, gu, wu, xb_h, dyb_h, residual_h, f2b_h, hidden_h, slope_h,
    rd, outb, du_h, dbr_h, dbrb_h, rowv_h, dbu_h,
    xb, dyb, residual, f2b, hidden, slope, du, dbr, dbrb, rowv, dbu,
    acc, psend, precv, gdv, guv, dup, osend, orecv, full, theirs,
    st, sb, ss, rs, ls, lsem, ps, pr, cs, msem,
):
    spot = place()
    x, k, y = spot
    is_a = k == y
    width = wd.shape[0]
    greet(Scatter.peers(spot))
    ring = Scatter(dd, rd, None, st, sb, None, ss, rs, ls, spot)
    ring.first()
    got_d = load_weight(wd, gd, gdv, lsem.at[0], k, is_a)
    moves = Moves(msem)
    got = [moves.start(a, b) for a, b in ((dyb_h, dyb), (slope_h, slope))]
    got_u = load_weight(wu, gu, guv, lsem.at[1], k, is_a)
    more = [
        moves.start(a, b) for a, b in ((hidden_h, hidden), (f2b_h, f2b), (residual_h, residual), (xb_h, xb))
    ]
    got_d()
    for c in got:
        c.wait()

    def contract(c, n):
        cols = pl.ds(c, n)
        grad = (nn(dyb[...], gdv[:, cols]) * slope[:, cols].astype(F32)).astype(BF)
        dup[:, cols] = grad
        dbu[:, cols] = jnp.sum(grad.astype(F32), axis=0, keepdims=True)

    chunks(slope.shape[1], 256, contract)
    got_u()
    for c in more:
        c.wait()
    tail = [pltpu.make_async_copy(a, b, msem.at[6 + i]) for i, (a, b) in enumerate(
        ((du, du_h), (dbr, dbr_h), (dbrb, dbrb_h), (rowv, rowv_h), (dbu, dbu_h)))]

    def second_grad(c, n):
        rows = pl.ds(c, n)
        psend[:, rows] = nt(dup[...], guv[rows, :]).astype(BF)

    chunks(psend.shape[1], 384, second_grad)
    exchange = remote(psend, precv, ps.at[0], pr.at[0], at(x, 1 - k, y))
    exchange.start()
    low = k == 0
    bd = xb[SEQ - 1 : PADS, :].astype(F32)[6:7]

    def side(a, i):
        lo = 2 * i * width
        return jnp.where(low, a[:, lo : lo + width], a[:, lo + width : lo + 2 * width])

    def down(c, n):
        rows = pl.ds(c, n)
        full[:, rows] = nt(hidden[...], gdv[rows, :])

    chunks(4 * width, 384, down)

    def far(a, i):
        lo = 2 * i * width
        return jnp.where(low, a[:, lo + width : lo + 2 * width], a[:, lo : lo + width])

    for i in range(2):
        osend[i] = far(full, i).astype(BF)
    outs = remote(osend, orecv, ps.at[1], pr.at[1], at(x, 1 - k, y))
    outs.start()
    ring.second()
    outs.wait_recv()
    for i in range(2):
        theirs[i] = (side(full, i) + side(residual, i) + side(bd, i) + orecv[i].astype(F32)).astype(BF)
    mine = pltpu.make_async_copy(theirs.at[0], outb.at[x], cs)
    mine.start()
    away = remote(theirs.at[1], outb.at[x], ps.at[2], pr.at[2], at(1 - x, k, y))
    away.start()

    def up_grad(j, carry):
        du[j] = tn(f2b[j], dup[...]).astype(BF)
        return carry

    lax.fori_loop(0, 4, up_grad, 0)
    tail[0].start()
    exchange.wait_recv()
    g2 = xb[SEQ - 1 : PADS, :].astype(F32)[2:3]
    acc[...] = jnp.zeros_like(acc)

    def norm2(r, n):
        rows = pl.ds(r, n)
        back, normed, incoming = norm_back_rows(residual[rows, :], psend[rows, :], precv[rows, :], g2)
        dyr = dyb[rows, :].astype(F32)
        low = (dyr + back).astype(BF)
        dbr[rows, :] = low
        fold(acc, 0, incoming * normed)
        fold(acc, 1, incoming)
        fold(acc, 2, low.astype(F32))
        fold(acc, 3, dyr)

    chunks(PADS, 128, norm2)
    rowv[...] = jnp.concatenate(
        [jnp.sum(acc[i], axis=0, keepdims=True) for i in range(4)] + [jnp.zeros((4, 4 * width), F32)], axis=0
    )
    for j in range(4):
        dbrb[j] = dbr[:, j * width : (j + 1) * width]
    for c in tail[1:]:
        c.start()
    ring.settle()
    mine.wait()
    remote(theirs.at[1], outb.at[1 - x], ps.at[2], pr.at[2], at(1 - x, k, y)).wait_recv()
    exchange.wait_send()
    outs.wait_send()
    away.wait_send()
    ring.close(home=False)
    for c in tail:
        c.wait()


def middle(dd, gd, wd, gu, wu, xb, dyb, residual, f2b, hidden, slope):
    width, ff = wd.shape
    anyspec = pl.BlockSpec(memory_space=pl.ANY)
    shape = jax.ShapeDtypeStruct
    dma = pltpu.SemaphoreType.DMA
    outs = [
        shape((5, width, ff), BF), shape((2, PADS, width), BF),
        shape((4, width, ff), BF), shape((PADS, 4 * width), BF), shape((4, PADS, width), BF),
        shape((8, 4 * width), F32), shape((1, ff), F32),
    ]
    return pl.pallas_call(
        middle_kernel,
        out_shape=outs,
        in_specs=[anyspec] * 11,
        out_specs=[anyspec] * len(outs),
        scratch_shapes=[
            *(pltpu.VMEM(a.shape, a.dtype) for a in (xb, dyb, residual, f2b, hidden, slope)),
            *(pltpu.VMEM(o.shape, o.dtype) for o in outs[2:]),
            pltpu.VMEM((4, 8, 4 * width), F32), pltpu.VMEM((PADS, 4 * width), BF), pltpu.VMEM((PADS, 4 * width), BF),
            pltpu.VMEM((4 * width, ff), BF), pltpu.VMEM((4 * width, ff), BF), pltpu.VMEM((PADS, ff), BF),
            pltpu.VMEM((2, PADS, width), BF), pltpu.VMEM((2, PADS, width), BF),
            pltpu.VMEM((PADS, 4 * width), F32), pltpu.VMEM((2, PADS, width), BF),
            pltpu.VMEM((3, width, ff), BF), pltpu.VMEM((width, ff), BF), dma((4,)), dma((6,)), dma((6,)),
            dma((2, 4)), dma((3,)), dma((3,)), dma(()), dma((11,)),
        ],
        compiler_params=pltpu.CompilerParams(collective_id=1, has_side_effects=True, vmem_limit_bytes=VMEM_CAP),
        name="middle",
    )(dd, gd, wd, gu, wu, xb, dyb, residual, f2b, hidden, slope)


class DpSum:
    def __init__(self, zs, zr, buf, out, ss, rs, ls):
        self.zs, self.zr, self.buf, self.out, self.ls = zs, zr, buf, out, ls
        size = lax.axis_size("dp")
        self.me = lax.axis_index("dp")
        self.copies = []
        for o in range(1, size):
            dest = lax.rem(self.me + o, size)
            self.copies.append(remote(zs.at[dest], zr.at[o - 1], ss.at[o - 1], rs.at[o - 1], {"dp": dest}))

    def start(self):
        for c in self.copies:
            c.start()

    def finish(self):
        for c in self.copies:
            c.wait_recv()
        sources = [self.zs.at[self.me]] + [self.zr.at[i] for i in range(len(self.copies))]
        for i, src in enumerate(sources):
            pltpu.make_async_copy(src, self.buf.at[i], self.ls.at[i]).start()
        for i, src in enumerate(sources):
            pltpu.make_async_copy(src, self.buf.at[i], self.ls.at[i]).wait()
        buf, out = self.buf, self.out

        def add(c, n):
            cols = pl.ds(c, n)
            out[:, cols] = sum(buf[i, :, cols].astype(F32) for i in range(len(sources)))

        chunks(out.shape[1], 128, add)

    def close(self):
        for c in self.copies:
            c.wait_send()


def backward_kernel(
    du, dd, rd, go, wo, gq, wq, xb_h, f1b_h, hflat_h, qh_h, oh_h, lse_h, dbr_h, dbrb_h, vec2_h, dbu_h,
    zsd, ru, zsu, ro, zso, ra, zsa, rb, zsb, zrd, zru, zro, zra, zrb, gin,
    td, tu, to, ta, tb, rowt, colt,
    xb, f1b, hflat, qh, oh, lse, dbr, dbrb, vec2, dbu,
    acc, gov, gqv, dh, dqh, dqkv, ps, pr, do, dq, home,
    stu, sbu, cvu, ssu, rsu, lsu, sto, sbo, cvo, sso, rso, lso,
    sta, sba, cva, ssa, rsa, lsa, stb, sbb, cvb, ssb, rsb, lsb, ssd, rsd,
    rowb, colv, rr, cr, rsum, csum, rz, cz, lsem, zss, zrs, zls, es, er, hs, hr, cs, vs, vr, ws, wr, msem,
):
    spot = place()
    x, k, y = spot
    is_a, is_b = k == y, k != y
    width, hw = xb.shape[1] // 4, hflat.shape[1]
    heads = hw // HD
    size, me = lax.axis_size("dp"), lax.axis_index("dp")
    summed = cvu.shape[1] > 1
    plane = [at(1 - x, k, y), at(x, k, 1 - y), at(1 - x, k, 1 - y)]
    plane += [at(x, 1 - k, y), at(1 - x, 1 - k, y), at(x, 1 - k, 1 - y), at(1 - x, 1 - k, 1 - y)]
    greet(plane + [{"dp": lax.rem(me + o, size)} for o in range(1, size)])
    side = jnp.where(is_a, 0, 1)
    row_sends = [
        remote(rowb.at[k if i == 1 else 2 + k], rr.at[i], vs.at[i], vr.at[i], plane[i]) for i in range(3)
    ]
    col_sends = [
        remote(colv, cr.at[side], vs.at[3], vr.at[3 + side], at(x, 1 - k, k)),
        remote(colv, cr.at[2 + side], vs.at[4], vr.at[5 + side], at(1 - x, k, k)),
        remote(colv, cr.at[2 + side], vs.at[5], vr.at[5 + side], at(1 - x, 1 - k, k)),
    ]
    col_extra = remote(colv, cr.at[1], vs.at[6], vr.at[4], at(x, k, k))
    dp_sends = []
    for o in range(1, size):
        dest = {"dp": lax.rem(me + o, size)}
        dp_sends.append(remote(rsum, rz.at[o - 1], ws.at[0, o - 1], wr.at[0, o - 1], dest))
        dp_sends.append(remote(csum, cz.at[o - 1], ws.at[1, o - 1], wr.at[1, o - 1], dest))
    ring_u = Scatter(du, ru, zsu, stu, sbu, cvu, ssu, rsu, lsu, spot)
    ring_u.first()
    moves = Moves(msem)
    got = [moves.start(a, b) for a, b in ((dbr_h, dbr), (hflat_h, hflat), (dbrb_h, dbrb))]
    got_o = load_weight(wo, go, gov, lsem.at[0], k, is_a)
    more = [
        moves.start(a, b)
        for a, b in ((qh_h, qh), (oh_h, oh), (lse_h, lse), (f1b_h, f1b), (xb_h, xb), (vec2_h, vec2), (dbu_h, dbu))
    ]
    got_q = load_weight(wq, gq, gqv, lsem.at[1], k, is_a)
    ring_d = Scatter(dd, rd, zsd, stu, sbu, cvu, ssd, rsd, lsu, spot)
    ring_o = Scatter(do, ro, zso, sto, sbo, cvo, sso, rso, lso, spot)
    ring_a = Scatter(dq.at[0], ra, zsa, sta, sba, cva, ssa, rsa, lsa, spot)
    ring_b = Scatter(dq.at[1], rb, zsb, stb, sbb, cvb, ssb, rsb, lsb, spot)
    if summed:
        sums = [
            DpSum(zs, zr, cv.at[0], t, zss.at[i], zrs.at[i], zls.at[i])
            for i, (zs, zr, cv, t) in enumerate(
                ((zsd, zrd, cvu, td), (zsu, zru, cvu, tu), (zso, zro, cvo, to), (zsa, zra, cva, ta), (zsb, zrb, cvb, tb))
            )
        ]
    dh[...] = jnp.zeros_like(dh)
    for c in got:
        c.wait()
    got_o()
    dqkv[:, 0:hw] = nn(dbr[...], gov[...]).astype(BF)
    for h in range(heads):
        dh[h, :, 0:HD] = dqkv[:, h * HD : (h + 1) * HD]

    def out_grad(j, carry):
        do[j] = tn(hflat[...], dbrb[j]).astype(BF)
        return carry

    lax.fori_loop(0, 4, out_grad, 0)
    ring_o.first()
    for c in more:
        c.wait()
    keymask = jnp.where(lax.broadcasted_iota(jnp.int32, (PADS, 1), 0) < SEQ, 0.0, -1e30)
    ones = jnp.ones((8, 128), F32)

    def attend(h, carry):
        q, kk, v, g = qh[h], qh[heads + h], qh[2 * heads + h], dh[h]
        p = jnp.exp(nt(kk, q) * HD ** (-0.5) + keymask - lse[pl.ds(h, 1), :])
        delta = lax.dot_general(
            ones, g.astype(F32) * oh[h].astype(F32), (((1,), (1,)), ((), ())),
            precision=lax.Precision.HIGHEST, preferred_element_type=F32,
        )[0:1]
        ds = (p * (nt(v, g) - delta)).astype(BF)
        dqh[2 * heads + h] = nn(p.astype(BF), g).astype(BF)
        dqh[heads + h] = (nn(ds, q) * HD ** (-0.5)).astype(BF)
        dqh[h] = (tn(kk, ds) * HD ** (-0.5)).T.astype(BF)
        return carry

    half_cols, group = dq.shape[3], heads // 2

    def one_half(half, carry):
        lax.fori_loop(half * group, (half + 1) * group, attend, 0)
        cols = pl.ds(pl.multiple_of(half * half_cols, 128), half_cols)
        block = dqkv.at[:, cols]
        for p in range(3):
            for i in range(group):
                lo = (p * group + i) * HD
                block[:, lo : lo + HD] = dqh[p * heads + half * group + i, :, 0:HD]
        block[:, 3 * group * HD :] = jnp.zeros((PADS, half_cols - 3 * group * HD), BF)

        def qkv_grad(j, c):
            dq[half, j] = tn(f1b[j], block[...]).astype(BF)
            return c

        lax.fori_loop(0, 4, qkv_grad, 0)

        @pl.when(half == 0)
        def _():
            ring_u.second()
            ring_a.first()
            ring_d.third(settled=True)
            ring_d.fourth()
            if summed:
                sums[0].start()

        return carry

    lax.fori_loop(0, 2, one_half, 0)
    ring_b.first()
    ring_o.second()
    got_q()

    def first_grad(c, n):
        rows = pl.ds(c, n)
        ps[:, rows] = nt(dqkv[...], gqv[rows, :]).astype(BF)

    chunks(ps.shape[1], 384, first_grad)
    exchange = remote(ps, pr, es, er, at(x, 1 - k, y))
    exchange.start()
    ring_d.home_sent()
    ring_u.third()
    ring_u.fourth()
    ring_a.second()
    if summed:
        sums[1].start()

    def bias_grad(c, n):
        cols = pl.ds(c, n)
        colv[0:1, cols] = jnp.sum(dqkv[:, cols].astype(F32), axis=0, keepdims=True)

    chunks(dqkv.shape[1], 128, bias_grad)
    colv[1:2, :] = dbu[...]
    exchange.wait_recv()
    exchange.wait_send()
    g1 = xb[SEQ - 1 : PADS, :].astype(F32)[1:2]
    acc[...] = jnp.zeros_like(acc)

    def norm1(r, n):
        rows = pl.ds(r, n)
        back, normed, incoming = norm_back_rows(xb[rows, :].astype(F32), ps[rows, :], pr[rows, :], g1)
        ps[rows, :] = (dbr[rows, :].astype(F32) + back).astype(BF)
        fold(acc, 0, incoming * normed)
        fold(acc, 1, incoming)

    chunks(PADS, 128, norm1)
    gain, shift = (jnp.sum(acc[i], axis=0, keepdims=True) for i in range(2))
    rows6 = jnp.concatenate(
        [gain, vec2[0:1], shift, vec2[1:2], vec2[2:3], vec2[3:4], jnp.zeros((2, 4 * width), F32)], axis=0
    )
    for j in range(4):
        rowb[j] = rows6[:, j * width : (j + 1) * width]
    for c in row_sends + col_sends:
        c.start()
    pl.when(is_b)(col_extra.start)
    low = k == 0
    for i in range(2):
        lo = 2 * i * width
        home[i] = jnp.where(low, ps[:, lo : lo + width], ps[:, lo + width : lo + 2 * width])
    mine = pltpu.make_async_copy(home.at[0], gin.at[x], cs)
    mine.start()
    away = remote(home.at[1], gin.at[x], hs, hr, at(1 - x, k, y))
    away.start()
    ring_b.second()
    ring_o.third()
    ring_o.fourth()
    if summed:
        sums[0].finish()
        sums[2].start()
    ring_a.third()
    ring_a.fourth()
    if summed:
        sums[3].start()
    for c in row_sends:
        c.wait_recv()
    for i in range(1, 4):
        remote(colv, cr.at[i], vs.at[3], vr.at[3 + i], at(x, 1 - k, k)).wait_recv()
    pl.when(is_b)(lambda: remote(colv, cr.at[0], vs.at[3], vr.at[3], at(x, 1 - k, k)).wait_recv())
    rsum[...] = rowb[k] + rr[0] + rr[1] + rr[2]

    @pl.when(is_a)
    def _():
        csum[...] = colv[...] + cr[1] + cr[2] + cr[3]

    @pl.when(is_b)
    def _():
        csum[...] = cr[0] + cr[1] + cr[2] + cr[3]

    for c in dp_sends:
        c.start()
    ring_b.third()
    ring_b.fourth()
    if summed:
        sums[4].start()
        sums[1].finish()
    mine.wait()
    remote(home.at[1], gin.at[1 - x], hs, hr, at(1 - x, k, y)).wait_recv()
    away.wait_send()
    for ring in (ring_u, ring_o, ring_a, ring_b):
        ring.close()
    for c in row_sends + col_sends:
        c.wait_send()
    pl.when(is_b)(col_extra.wait_send)
    for c in dp_sends:
        c.wait_recv()
        c.wait_send()
    rowt[...] = rsum[...] + sum(rz[o] for o in range(size - 1))
    colt[...] = csum[...] + sum(cz[o] for o in range(size - 1))
    if summed:
        for total in sums[2:]:
            total.finish()
        for total in sums:
            total.close()


def backward(parts, du, dd, rd, go, wo, gq, wq, xb, f1b, hflat, qh, oh, lse, dbr, dbrb, vec2, dbu):
    width, ff = du.shape[1:]
    hw, nq = wo.shape[1], wq.shape[1]
    full, heads = 4 * width, hw // HD
    anyspec = pl.BlockSpec(memory_space=pl.ANY)
    vspec = pl.BlockSpec(memory_space=pltpu.VMEM)
    shape = jax.ShapeDtypeStruct
    dma = pltpu.SemaphoreType.DMA
    others = max(parts - 1, 1)
    peers = lax.axis_size("dp") - 1
    piece, slab = width // parts, hw // parts
    nh = nq // 2
    outs = [
        shape((parts, piece, ff), BF), shape((5, width, ff), BF), shape((parts, piece, ff), BF),
        shape((5, hw, width), BF), shape((parts, slab, width), BF),
        shape((5, width, nh), BF), shape((parts, piece, nh), BF), shape((5, width, nh), BF), shape((parts, piece, nh), BF),
        shape((others, piece, ff), BF), shape((others, piece, ff), BF), shape((others, slab, width), BF),
        shape((others, piece, nh), BF), shape((others, piece, nh), BF), shape((2, PADS, width), BF),
        *(
            shape(d if parts > 1 else (8, 128), F32)
            for d in ((piece, ff), (piece, ff), (slab, width), (piece, nh), (piece, nh))
        ),
        shape((8, width), F32), shape((2, ff), F32),
    ]
    return pl.pallas_call(
        backward_kernel,
        out_shape=outs,
        in_specs=[anyspec] * 17,
        out_specs=[anyspec] * 15 + [vspec] * 7,
        scratch_shapes=[pltpu.VMEM(a.shape, a.dtype) for a in (xb, f1b, hflat, qh, oh, lse, dbr, dbrb, vec2, dbu)]
        + [
            pltpu.VMEM((2, 8, full), F32), pltpu.VMEM((full, hw), BF), pltpu.VMEM((full, nq), BF),
            pltpu.VMEM((heads, PADS, 128), BF), pltpu.VMEM((3 * heads, PADS, 128), BF), pltpu.VMEM((PADS, nq), BF),
            pltpu.VMEM((PADS, full), BF), pltpu.VMEM((PADS, full), BF),
            pltpu.VMEM((4, hw, width), BF), pltpu.VMEM((2, 4, width, nh), BF), pltpu.VMEM((2, PADS, width), BF),
        ]
        + scatter_scratch(width, ff, parts) + scatter_scratch(hw, width, parts)
        + scatter_scratch(width, nh, parts) + scatter_scratch(width, nh, parts) + [dma((4,)), dma((6,))]
        + [
            pltpu.VMEM((4, 8, width), F32), pltpu.VMEM((2, ff), F32), pltpu.VMEM((3, 8, width), F32), pltpu.VMEM((4, 2, ff), F32),
            pltpu.VMEM((8, width), F32), pltpu.VMEM((2, ff), F32), pltpu.VMEM((peers, 8, width), F32), pltpu.VMEM((peers, 2, ff), F32),
        ]
        + [dma((2, 4)), dma((5, others)), dma((5, others)), dma((5, others + 1)), dma(()), dma(()), dma(()), dma(()), dma(()),
           dma((7,)), dma((7,)), dma((2, peers)), dma((2, peers)), dma((10,))],
        compiler_params=pltpu.CompilerParams(collective_id=2, has_side_effects=True, vmem_limit_bytes=VMEM_CAP),
        name="backward",
    )(du, dd, rd, go, wo, gq, wq, xb, f1b, hflat, qh, oh, lse, dbr, dbrb, vec2, dbu)


def shards(tokens, ln_gain, ln_bias, w_qkv, b_qv, w_out, b_out, w_up, b_up, w_down, b_down, cotangent):
    width = tokens.shape[1]
    hw = b_qv.shape[1]

    extra = jnp.concatenate(
        [ln_gain, ln_bias, b_out[None], b_down[None], jnp.zeros((1, width), BF)], axis=0
    )
    images = tokens.shape[0] // SEQ
    blank = jnp.zeros((PADS - SEQ, width), BF)

    def with_rows(a, tail):
        return jnp.stack([jnp.concatenate([a[i * SEQ : (i + 1) * SEQ], tail]) for i in range(images)])

    tok2, cot2 = with_rows(tokens, extra), with_rows(cotangent, blank)
    ff = b_up.shape[0]
    nq, hh = padded(hw), hw // 2
    gap = jnp.zeros((nq // 2 - 3 * hh,), BF)
    nil = jnp.zeros((hh,), BF)
    bqkv = jnp.concatenate(
        [b_qv[0, :hh], nil, b_qv[1, :hh], gap, b_qv[0, hh:], nil, b_qv[1, hh:], gap, jnp.zeros((ff - nq,), BF)]
    )
    bias = jnp.concatenate([bqkv[None], b_up[None], jnp.zeros((14, ff), BF)])
    side = jnp.zeros((width, gap.shape[0]), BF)
    qblock = jnp.concatenate(
        [w_qkv[:, p, i * hh : (i + 1) * hh] if p < 3 else side for i in range(2) for p in range(4)], axis=1
    )
    wot, wdt = w_out.T, w_down.T
    gq, go, gu, gd, xb, dy, f1b, qh, oh, hflat, lse, residual, f2b, hidden, slope, dd = forward(
        tok2, cot2, bias, qblock, wot, w_up, wdt
    )
    dp_size = lax.axis_size("dp")
    parts = dp_size if width % dp_size == 0 and (width // dp_size) % 8 == 0 else 1
    rd, outb, du, dbr, dbrb, vec2, dbu = middle(dd, gd, wdt, gu, w_up, xb, dy, residual, f2b, hidden, slope)
    output = jnp.concatenate([outb[i, :SEQ] for i in range(images)])
    back = backward(parts, du, dd, rd, go, wot, gq, qblock, xb, f1b, hflat, qh, oh, lse, dbr, dbrb, vec2, dbu)
    zsd, _, zsu, _, zso, _, zsa, _, zsb = back[:9]
    gin, td, tu, to, ta, tb, rowt, colt = back[14:]
    input_grad = jnp.concatenate([gin[i, :SEQ] for i in range(images)])
    if parts == 1:

        def over_dp(a):
            return lax.psum_scatter(a[0], "dp", scatter_dimension=0, tiled=True).astype(F32)

        td, tu, to, ta, tb = (over_dp(a) for a in (zsd, zsu, zso, zsa, zsb))

    return (
        output,
        input_grad,
        rowt[0:2],
        rowt[2:4],
        jnp.concatenate([a[:, : 3 * hh].reshape(-1, 3, hh) for a in (ta, tb)], axis=2),
        jnp.stack(
            [jnp.concatenate([colt[0, i * nq // 2 + p * hh :][:hh] for i in range(2)]) for p in (0, 2)]
        ),
        to,
        rowt[4],
        tu,
        colt[1],
        td.T,
        rowt[5],
    )


def solution(mesh):
    placed = (
        P(("dp", "col"), "row"),
        P(None, "row"),
        P(None, "row"),
        P("row", None, "col"),
        P(None, "col"),
        P("col", "row"),
        P("row"),
        P("row", "col"),
        P("col"),
        P("col", "row"),
        P("row"),
        P(("dp", "col"), "row"),
    )
    return jax.shard_map(
        shards,
        mesh=mesh,
        in_specs=placed,
        out_specs=(
            P(("dp", "col"), "row"),
            P(("dp", "col"), "row"),
            P(None, "row"),
            P(None, "row"),
            P(("row", "dp"), None, "col"),
            P(None, "col"),
            P(("col", "dp"), "row"),
            P("row"),
            P(("row", "dp"), "col"),
            P("col"),
            P("col", ("row", "dp")),
            P("row"),
        ),
        check_vma=False,
    )
```

profile of v0, /device:TPU:0, one launch (start us, length us, event | category | flops | bytes accessed | tf_op | source)
XLA Modules:
  0.0 382.3 jit_solution(7813933303249960761)
XLA Ops:
  0.7 0.1 pad.16.clone
  0.7 0.7 broadcast_in_dim.31
  1.5 0.7 broadcast_in_dim.32
  2.2 0.9 slice_reduce_fusion.7
  3.1 0.1 concatenate.43
  3.2 0.7 broadcast_in_dim.38
  3.9 0.7 maximum_maximum_fusion.bias
  4.6 1.0 slice.110
  5.7 0.0 copy-start.12
  5.7 0.3 copy.41
  6.0 0.2 slice.111
  6.2 0.3 copy.42
  6.5 0.3 pad_bitcast_fusion
  6.8 1.2 pad_maximum_fusion.1.cot
  8.0 0.2 fusion
  8.2 0.3 copy.39
  8.6 0.2 copy-done.10
  8.7 0.0 copy-done.11
  8.7 0.9 concatenate.39
  9.6 0.3 copy.40
  9.9 0.0 copy-start
  9.9 0.9 concatenate.40
  10.8 1.2 pad_maximum_fusion.tok
  12.1 0.3 slice_bitcast_fusion.4
  12.4 2.0 concatenate.45.wq
  14.4 156.2 %forward.1 = (bf16[4,288,1792]{2,1,0:T(8,128)(2,1)}, bf16[4,288,576]{2,1,0:T(8,128)(2,1)}, bf16[4,288,2152]{2,1,0:T(8,128)(2,1)}, bf16[4,288,2152]{2,1,0:T(8,128...) custom-call(bf16[2,736,288]{2,1,0:T(8,128)(2,1)} %pad_maximum_fusion, ...), custom_call_target="tpu_custom_call" | custom-call | tf_op jit(solution)/shard_map/forward/pallas_call | solution.py:342
  170.6 60.2 %middle.1 = (bf16[5,288,2152]{2,1,0:T(8,128)(2,1)}, bf16[2,736,288]{2,1,0:T(8,128)(2,1)}, bf16[4,288,2152]{2,1,0:T(8,128)(2,1)}, bf16[736,1152]{1,0:T(8,128)(2,1...) custom-call(bf16[4,288,2152]{2,1,0:T(8,128)(2,1)} %get-tuple-element.43.dd, ...), custom_call_target="tpu_custom_call" | custom-call | tf_op jit(solution)/shard_map/middle/pallas_call | solution.py:641
  230.8 1.3 slice_bitcast_fusion.3
  232.2 0.2 pad_maximum_fusion.2
  232.4 1.9 copy.36
  234.3 137.7 %backward.1 = (bf16[4,72,2152]{2,1,0:T(8,128)(2,1)}, bf16[5,288,2152]{2,1,0:T(8,128)(2,1)}, bf16[4,72,2152]{2,1,0:T(8,128)(2,1)}, bf16[5,576,288]{2,1,0:T(8,128)...) custom-call(bf16[4,288,2152]{2,1,0:T(8,128)(2,1)} %get-tuple-element, ...), custom_call_target="tpu_custom_call" | custom-call | tf_op jit(solution)/shard_map/backward/pallas_call | solution.py:944
  372.0 1.3 slice_bitcast_fusion.1
  373.4 0.2 pad_maximum_fusion.3
  373.6 1.9 copy.37
  375.6 0.6 slice_reduce_fusion.1
  376.2 0.6 fusion.1
  376.7 0.1 slice_reduce_fusion.6
  376.8 0.6 slice_reduce_fusion
  377.5 0.1 pad_maximum_fusion.6
  377.5 0.1 pad_maximum_fusion.7
  377.6 0.6 pad_maximum_fusion.5
  378.2 0.2 reshape.34
  378.5 0.2 reshape.35
  378.8 0.3 pad_maximum_fusion.4
  379.1 0.8 copy.38
  379.9 0.7 copy.46
  380.6 0.8 copy.47
  381.4 0.8 copy.48
  (31 shorter events, 0.1 us)
Async XLA Ops:
  0.6 5.4 %copy-start.1 = (bf16[1458,288]{0,1:T(8,128)(2,1)S(1)}, bf16[1458,288]{0,1:T(8,128)(2,1)}, u32[]{:S(2)}) copy-start(bf16[1458,288]{0,1:T(8,128)(2,1)} %param.23) | copy-start | bytes 2519428
  5.7 0.8 copy-start.12
  6.8 1.3 copy-start.2
  8.0 0.7 copy-start.10
  8.0 0.7 copy-start.11
  9.9 2.2 copy-start
  373.6 2.0 copy-start.9
  373.6 3.1 copy-start.8
  373.6 4.6 %copy-start.6 = (f32[72,896]{1,0:T(8,128)S(1)}, f32[72,896]{1,0:T(8,128)}, u32[]{:S(2)}) copy-start(f32[72,896]{1,0:T(8,128)} %get-tuple-element.68) | copy-start | bytes 774148
  373.6 4.9 %copy-start.5 = (f32[72,896]{1,0:T(8,128)S(1)}, f32[72,896]{1,0:T(8,128)}, u32[]{:S(2)}) copy-start(f32[72,896]{1,0:T(8,128)} %get-tuple-element.69) | copy-start | bytes 774148
  378.7 1.2 copy-start.7
  378.8 1.8 copy-start.4
  379.1 2.4 copy-start.3
where the time goes:
time: 385 us; the launch traced here: 382 us
  Pallas kernels  354 us (92%)
  local copies, waits for them, and re-layouts  22.3 us (6%)
  other arithmetic  4.92 us (1%)
    pallas_call x1, Pallas kernels, forward(): pl.pallas_call(forward_kernel, out_shape=outs, in_specs=[anyspec] * 7, ou...  156 us
    pallas_call x1, Pallas kernels, backward(): pl.pallas_call(backward_kernel, out_shape=outs, in_specs=[anyspec] * 17,...  138 us
    pallas_call x1, Pallas kernels, middle(): pl.pallas_call(middle_kernel, out_shape=outs, in_specs=[anyspec] * 11, ou...  60.2 us
    unnamed x36, local copies, waits for them, and re-layouts  8.42 us

commit v1 on v0

--- a/solution.py
+++ b/solution.py
@@ -1,3 +1,5 @@
+import types
+
 import jax
 import jax.numpy as jnp
 from jax import lax
@@ -84,25 +86,17 @@
             c.wait()
 
 
-def forward_kernel(
+def forward_phase(
     tok, cot, bias, wq, wo, wu, wd,
     gq, go, gu, gd, xb_h, dyb_h, f1b_h, qh_h, oh_h, hflat_h, lse_h, residual_h, f2b_h, hidden_h, slope_h, dd_h,
-    xb, dyb, bv, f1b, qh, oh, hflat, lse, residual, f2b, hidden, slope, dd,
-    tbuf, cbuf, gqv, gov, guv, f1, psend, precv,
-    ssem, rsem, csem, lsem, wsend, wrecv, msem,
+    tbuf, cbuf, bv, precv, ssem, rsem, csem, lsem, wsend, wrecv, msem, spot, after,
+    xb, dyb, f1b, qh, oh, hflat, lse, residual, f2b, hidden, slope, dd, tb, gqv, gov, guv, f1, psend,
 ):
-    x, k, y = place()
+    x, k, y = spot
     is_a, is_b = k == y, k != y
     hw = hflat.shape[1]
     heads = hw // HD
     width = tok.shape[2]
-    greet([at(x, 1 - k, y), at(1 - x, k, y), at(1 - x, 1 - k, y), at(x, k, 1 - y), at(x, 1 - k, 1 - y)])
-
-    def remote(src, dst, s, r, dest):
-        return pltpu.make_async_remote_copy(
-            src_ref=src, dst_ref=dst, send_sem=s, recv_sem=r, device_id=dest, device_id_type=MESH
-        )
-
     blocks, wholes = (wq, wo, wu, wd), (gq, go, gu, gd)
     out = Moves(msem)
 
@@ -187,25 +181,30 @@
     c2 = remote(cbuf.at[2 + k], cbuf.at[2 + k], ssem.at[5], rsem.at[5], at(x, 1 - k, y))
     bs = remote(bias, bv, ssem.at[6], rsem.at[6], at(x, k, 1 - y))
     pe = remote(psend, precv, ssem.at[7], rsem.at[7], at(x, 1 - k, y))
-    tl = pltpu.make_async_copy(tok.at[x], tbuf.at[k], csem.at[0])
-    cl = pltpu.make_async_copy(cot.at[x], cbuf.at[k], csem.at[1])
+
+    def collect(src, buf, wide):
+        parts = [(src.at[x], k), (buf.at[1 - k], 1 - k), (buf.at[2], 2), (buf.at[3], 3)]
+        copies = [pltpu.make_async_copy(a, tb.at[j], lsem.at[i]) for i, (a, j) in enumerate(parts)]
+        for c in copies:
+            c.start()
+        for c in copies:
+            c.wait()
+        for j in range(4):
+            wide[:, j * width : (j + 1) * width] = tb[j]
+
     bl = pltpu.make_async_copy(bias, bv, csem.at[2])
 
     tx.start()
     t1.start()
-    tl.start()
     start_own(0)
     both(lambda: (bl.start(), bs.start()) and None, lambda: None)
-    cl.start()
     c1.start()
 
     tx.wait_recv()
     t2.start()
-    tl.wait()
     t1.wait_recv()
     t2.wait_recv()
-    for j in range(4):
-        xb[:, j * width : (j + 1) * width] = tbuf[j]
+    collect(tok, tbuf, xb)
     vecs = xb[SEQ - 1 : PADS, :].astype(F32)
     g1, g2, s1, s2, bo = (vecs[j : j + 1] for j in range(1, 6))
 
@@ -302,59 +301,26 @@
     out.start(slope, slope_h)
     cx.wait_recv()
     c2.start()
-    cl.wait()
     c1.wait_recv()
     c2.wait_recv()
-    for j in range(4):
-        dyb[:, j * width : (j + 1) * width] = cbuf[j]
+    collect(cot, cbuf, dyb)
 
     def down_grad(j, carry):
-        dd[j] = tn(cbuf[j], hidden[...]).astype(BF)
+        dd[j] = tn(tb[j], hidden[...]).astype(BF)
         return carry
 
     out.start(dyb, dyb_h)
+    start_relay(3)
     lax.fori_loop(0, 4, down_grad, 0)
     out.start(dd, dd_h)
-    start_relay(3)
+    out.finish()
     wait_rest(3)
+    after()
     for c in (tx, cx, t1, c1, t2, c2, pe):
         c.wait_send()
     both(bs.wait_send, lambda: None)
     for w in range(4):
         finish_sends(w)
-    out.finish()
-
-
-def forward(tok, cot, bias, wq, wo, wu, wd):
-    width, hw, ff = tok.shape[2], wo.shape[1], wu.shape[1]
-    full = 4 * width
-    heads = hw // HD
-    anyspec = pl.BlockSpec(memory_space=pl.ANY)
-    shape = jax.ShapeDtypeStruct
-    outs = [
-        shape((4,) + wq.shape, BF), shape((4,) + wo.shape, BF), shape((4,) + wu.shape, BF), shape((4,) + wd.shape, BF),
-        shape((PADS, full), BF), shape((PADS, full), BF), shape((4, PADS, width), BF),
-        shape((3 * heads, PADS, 128), BF), shape((heads, PADS, 128), BF), shape((PADS, hw), BF), shape((heads, PADS), F32),
-        shape((PADS, full), F32), shape((4, PADS, width), BF), shape((PADS, ff), BF), shape((PADS, ff), BF),
-        shape((4, width, ff), BF),
-    ]
-    dma = pltpu.SemaphoreType.DMA
-    return pl.pallas_call(
-        forward_kernel,
-        out_shape=outs,
-        in_specs=[anyspec] * 7,
-        out_specs=[anyspec] * len(outs),
-        scratch_shapes=[pltpu.VMEM(o.shape, o.dtype) for o in outs[4:6]] + [pltpu.VMEM(bias.shape, BF)]
-        + [pltpu.VMEM(o.shape, o.dtype) for o in outs[6:]]
-        + [
-            pltpu.VMEM((4, PADS, width), BF), pltpu.VMEM((4, PADS, width), BF),
-            pltpu.VMEM((full, wq.shape[1]), BF), pltpu.VMEM((full, hw), BF), pltpu.VMEM((full, ff), BF),
-            pltpu.VMEM((PADS, full), BF), pltpu.VMEM((PADS, full), BF), pltpu.VMEM((PADS, full), BF),
-            dma((8,)), dma((8,)), dma((3,)), dma((4,)), dma((4, 4)), dma((4, 4)), dma((12,)),
-        ],
-        compiler_params=pltpu.CompilerParams(collective_id=0, has_side_effects=True, vmem_limit_bytes=VMEM_CAP),
-        name="forward",
-    )(tok, cot, bias, wq, wo, wu, wd)
 
 
 def load_weight(b, g, dst, sem, k, is_a):
@@ -390,8 +356,9 @@
         self.x1 = remote(d.at[2], r.at[0], ss.at[0], rs.at[0], across)
         self.y1 = remote(d.at[3], r.at[1], ss.at[1], rs.at[1], over)
         self.y1b = remote(d.at[1], r.at[2], ss.at[2], rs.at[2], over)
-        self.x2 = remote(sb, r.at[3], ss.at[1], rs.at[3], across)
-        self.y2 = remote(sb, r.at[4], ss.at[3], rs.at[4], over)
+        if sb is not None:
+            self.x2 = remote(sb, r.at[3], ss.at[1], rs.at[3], across)
+            self.y2 = remote(sb, r.at[4], ss.at[3], rs.at[4], over)
         if zs is not None:
             self.home = remote(cv.at[1], zs, ss.at[2], rs.at[5], mate)
 
@@ -441,9 +408,8 @@
 
         pl.when(self.is_a)(a)
 
-    def third(self, settled=False):
-        if not settled:
-            self.settle()
+    def third(self):
+        self.settle()
         st, cv = self.st, self.cv
         parts, piece = cv.shape[1], cv.shape[2]
 
@@ -489,13 +455,6 @@
     def peers(spot):
         x, k, y = spot
         return [at(1 - x, k, y), at(x, k, 1 - y), at(x, 1 - k, y)]
-
-
-def scatter_scratch(rows, cols, parts):
-    return [
-        pltpu.VMEM((3, rows, cols), BF), pltpu.VMEM((rows, cols), BF), pltpu.VMEM((2, parts, rows // parts, cols), BF),
-        pltpu.SemaphoreType.DMA((4,)), pltpu.SemaphoreType.DMA((6,)), pltpu.SemaphoreType.DMA((6,)),
-    ]
 
 
 def norm_back_rows(values, mine, theirs, gain):
@@ -513,20 +472,17 @@
     acc[i] += sum(rows[8 * j : 8 * j + 8] for j in range(rows.shape[0] // 8))
 
 
-def middle_kernel(
+def middle_phase(
     dd, gd, wd, gu, wu, xb_h, dyb_h, residual_h, f2b_h, hidden_h, slope_h,
     rd, outb, du_h, dbr_h, dbrb_h, rowv_h, dbu_h,
+    precv, orecv, theirs, sb, ss, rs, ls, lsem, ps, pr, cs, msem, spot, after,
     xb, dyb, residual, f2b, hidden, slope, du, dbr, dbrb, rowv, dbu,
-    acc, psend, precv, gdv, guv, dup, osend, orecv, full, theirs,
-    st, sb, ss, rs, ls, lsem, ps, pr, cs, msem,
+    acc, psend, gdv, guv, dup, osend, full, st,
 ):
-    spot = place()
     x, k, y = spot
     is_a = k == y
     width = wd.shape[0]
-    greet(Scatter.peers(spot))
     ring = Scatter(dd, rd, None, st, sb, None, ss, rs, ls, spot)
-    ring.first()
     got_d = load_weight(wd, gd, gdv, lsem.at[0], k, is_a)
     moves = Moves(msem)
     got = [moves.start(a, b) for a, b in ((dyb_h, dyb), (slope_h, slope))]
@@ -551,6 +507,13 @@
     tail = [pltpu.make_async_copy(a, b, msem.at[6 + i]) for i, (a, b) in enumerate(
         ((du, du_h), (dbr, dbr_h), (dbrb, dbrb_h), (rowv, rowv_h), (dbu, dbu_h)))]
 
+    def up_grad(j, carry):
+        du[j] = tn(f2b[j], dup[...]).astype(BF)
+        return carry
+
+    lax.fori_loop(0, 4, up_grad, 0)
+    tail[0].start()
+
     def second_grad(c, n):
         rows = pl.ds(c, n)
         psend[:, rows] = nt(dup[...], guv[rows, :]).astype(BF)
@@ -558,6 +521,9 @@
     chunks(psend.shape[1], 384, second_grad)
     exchange = remote(psend, precv, ps.at[0], pr.at[0], at(x, 1 - k, y))
     exchange.start()
+    tail[0].wait()
+    ring.second()
+    after()
     low = k == 0
     bd = xb[SEQ - 1 : PADS, :].astype(F32)[6:7]
 
@@ -579,7 +545,6 @@
         osend[i] = far(full, i).astype(BF)
     outs = remote(osend, orecv, ps.at[1], pr.at[1], at(x, 1 - k, y))
     outs.start()
-    ring.second()
     outs.wait_recv()
     for i in range(2):
         theirs[i] = (side(full, i) + side(residual, i) + side(bd, i) + orecv[i].astype(F32)).astype(BF)
@@ -588,12 +553,6 @@
     away = remote(theirs.at[1], outb.at[x], ps.at[2], pr.at[2], at(1 - x, k, y))
     away.start()
 
-    def up_grad(j, carry):
-        du[j] = tn(f2b[j], dup[...]).astype(BF)
-        return carry
-
-    lax.fori_loop(0, 4, up_grad, 0)
-    tail[0].start()
     exchange.wait_recv()
     g2 = xb[SEQ - 1 : PADS, :].astype(F32)[2:3]
     acc[...] = jnp.zeros_like(acc)
@@ -617,45 +576,10 @@
         dbrb[j] = dbr[:, j * width : (j + 1) * width]
     for c in tail[1:]:
         c.start()
-    ring.settle()
-    mine.wait()
-    remote(theirs.at[1], outb.at[1 - x], ps.at[2], pr.at[2], at(1 - x, k, y)).wait_recv()
     exchange.wait_send()
     outs.wait_send()
-    away.wait_send()
-    ring.close(home=False)
-    for c in tail:
+    for c in tail[1:]:
         c.wait()
-
-
-def middle(dd, gd, wd, gu, wu, xb, dyb, residual, f2b, hidden, slope):
-    width, ff = wd.shape
-    anyspec = pl.BlockSpec(memory_space=pl.ANY)
-    shape = jax.ShapeDtypeStruct
-    dma = pltpu.SemaphoreType.DMA
-    outs = [
-        shape((5, width, ff), BF), shape((2, PADS, width), BF),
-        shape((4, width, ff), BF), shape((PADS, 4 * width), BF), shape((4, PADS, width), BF),
-        shape((8, 4 * width), F32), shape((1, ff), F32),
-    ]
-    return pl.pallas_call(
-        middle_kernel,
-        out_shape=outs,
-        in_specs=[anyspec] * 11,
-        out_specs=[anyspec] * len(outs),
-        scratch_shapes=[
-            *(pltpu.VMEM(a.shape, a.dtype) for a in (xb, dyb, residual, f2b, hidden, slope)),
-            *(pltpu.VMEM(o.shape, o.dtype) for o in outs[2:]),
-            pltpu.VMEM((4, 8, 4 * width), F32), pltpu.VMEM((PADS, 4 * width), BF), pltpu.VMEM((PADS, 4 * width), BF),
-            pltpu.VMEM((4 * width, ff), BF), pltpu.VMEM((4 * width, ff), BF), pltpu.VMEM((PADS, ff), BF),
-            pltpu.VMEM((2, PADS, width), BF), pltpu.VMEM((2, PADS, width), BF),
-            pltpu.VMEM((PADS, 4 * width), F32), pltpu.VMEM((2, PADS, width), BF),
-            pltpu.VMEM((3, width, ff), BF), pltpu.VMEM((width, ff), BF), dma((4,)), dma((6,)), dma((6,)),
-            dma((2, 4)), dma((3,)), dma((3,)), dma(()), dma((11,)),
-        ],
-        compiler_params=pltpu.CompilerParams(collective_id=1, has_side_effects=True, vmem_limit_bytes=VMEM_CAP),
-        name="middle",
-    )(dd, gd, wd, gu, wu, xb, dyb, residual, f2b, hidden, slope)
 
 
 class DpSum:
@@ -693,17 +617,17 @@
             c.wait_send()
 
 
-def backward_kernel(
+def backward_phase(
     du, dd, rd, go, wo, gq, wq, xb_h, f1b_h, hflat_h, qh_h, oh_h, lse_h, dbr_h, dbrb_h, vec2_h, dbu_h,
     zsd, ru, zsu, ro, zso, ra, zsa, rb, zsb, zrd, zru, zro, zra, zrb, gin,
     td, tu, to, ta, tb, rowt, colt,
-    xb, f1b, hflat, qh, oh, lse, dbr, dbrb, vec2, dbu,
-    acc, gov, gqv, dh, dqh, dqkv, ps, pr, do, dq, home,
-    stu, sbu, cvu, ssu, rsu, lsu, sto, sbo, cvo, sso, rso, lso,
-    sta, sba, cva, ssa, rsa, lsa, stb, sbb, cvb, ssb, rsb, lsb, ssd, rsd,
-    rowb, colv, rr, cr, rsum, csum, rz, cz, lsem, zss, zrs, zls, es, er, hs, hr, cs, vs, vr, ws, wr, msem,
+    pr, sbd, rowb, colv, rr, cr, rsum, csum, rz, cz,
+    ssu, rsu, lsu, sso, rso, lso, ssa, rsa, lsa, ssb, rsb, lsb, ssd, rsd,
+    lsem, zss, zrs, zls, es, er, hs, hr, cs, vs, vr, ws, wr, msem, spot, later,
+    xb, f1b, hflat, dbr, dbrb, vec2, dbu,
+    acc, gov, dqkv, do, dq,
+    stu, sbu, cvu, sto, sbo, cvo, sta, sba, cva, sbb, cvb,
 ):
-    spot = place()
     x, k, y = spot
     is_a, is_b = k == y, k != y
     width, hw = xb.shape[1] // 4, hflat.shape[1]
@@ -711,8 +635,6 @@
     size, me = lax.axis_size("dp"), lax.axis_index("dp")
     summed = cvu.shape[1] > 1
     plane = [at(1 - x, k, y), at(x, k, 1 - y), at(1 - x, k, 1 - y)]
-    plane += [at(x, 1 - k, y), at(1 - x, 1 - k, y), at(x, 1 - k, 1 - y), at(1 - x, 1 - k, 1 - y)]
-    greet(plane + [{"dp": lax.rem(me + o, size)} for o in range(1, size)])
     side = jnp.where(is_a, 0, 1)
     row_sends = [
         remote(rowb.at[k if i == 1 else 2 + k], rr.at[i], vs.at[i], vr.at[i], plane[i]) for i in range(3)
@@ -729,19 +651,14 @@
         dp_sends.append(remote(rsum, rz.at[o - 1], ws.at[0, o - 1], wr.at[0, o - 1], dest))
         dp_sends.append(remote(csum, cz.at[o - 1], ws.at[1, o - 1], wr.at[1, o - 1], dest))
     ring_u = Scatter(du, ru, zsu, stu, sbu, cvu, ssu, rsu, lsu, spot)
-    ring_u.first()
     moves = Moves(msem)
     got = [moves.start(a, b) for a, b in ((dbr_h, dbr), (hflat_h, hflat), (dbrb_h, dbrb))]
     got_o = load_weight(wo, go, gov, lsem.at[0], k, is_a)
-    more = [
-        moves.start(a, b)
-        for a, b in ((qh_h, qh), (oh_h, oh), (lse_h, lse), (f1b_h, f1b), (xb_h, xb), (vec2_h, vec2), (dbu_h, dbu))
-    ]
-    got_q = load_weight(wq, gq, gqv, lsem.at[1], k, is_a)
-    ring_d = Scatter(dd, rd, zsd, stu, sbu, cvu, ssd, rsd, lsu, spot)
+    more = [moves.start(a, b) for a, b in ((f1b_h, f1b), (xb_h, xb), (vec2_h, vec2), (dbu_h, dbu))]
+    ring_d = Scatter(dd, rd, zsd, stu, sbd, cvu, ssd, rsd, lsu, spot)
     ring_o = Scatter(do, ro, zso, sto, sbo, cvo, sso, rso, lso, spot)
     ring_a = Scatter(dq.at[0], ra, zsa, sta, sba, cva, ssa, rsa, lsa, spot)
-    ring_b = Scatter(dq.at[1], rb, zsb, stb, sbb, cvb, ssb, rsb, lsb, spot)
+    ring_b = Scatter(dq.at[1], rb, zsb, sta, sbb, cvb, ssb, rsb, lsb, spot)
     if summed:
         sums = [
             DpSum(zs, zr, cv.at[0], t, zss.at[i], zrs.at[i], zls.at[i])
@@ -749,221 +666,304 @@
                 ((zsd, zrd, cvu, td), (zsu, zru, cvu, tu), (zso, zro, cvo, to), (zsa, zra, cva, ta), (zsb, zrb, cvb, tb))
             )
         ]
-    dh[...] = jnp.zeros_like(dh)
-    for c in got:
-        c.wait()
-    got_o()
-    dqkv[:, 0:hw] = nn(dbr[...], gov[...]).astype(BF)
-    for h in range(heads):
-        dh[h, :, 0:HD] = dqkv[:, h * HD : (h + 1) * HD]
-
-    def out_grad(j, carry):
-        do[j] = tn(hflat[...], dbrb[j]).astype(BF)
-        return carry
-
-    lax.fori_loop(0, 4, out_grad, 0)
-    ring_o.first()
-    for c in more:
-        c.wait()
-    keymask = jnp.where(lax.broadcasted_iota(jnp.int32, (PADS, 1), 0) < SEQ, 0.0, -1e30)
-    ones = jnp.ones((8, 128), F32)
-
-    def attend(h, carry):
-        q, kk, v, g = qh[h], qh[heads + h], qh[2 * heads + h], dh[h]
-        p = jnp.exp(nt(kk, q) * HD ** (-0.5) + keymask - lse[pl.ds(h, 1), :])
-        delta = lax.dot_general(
-            ones, g.astype(F32) * oh[h].astype(F32), (((1,), (1,)), ((), ())),
-            precision=lax.Precision.HIGHEST, preferred_element_type=F32,
-        )[0:1]
-        ds = (p * (nt(v, g) - delta)).astype(BF)
-        dqh[2 * heads + h] = nn(p.astype(BF), g).astype(BF)
-        dqh[heads + h] = (nn(ds, q) * HD ** (-0.5)).astype(BF)
-        dqh[h] = (tn(kk, ds) * HD ** (-0.5)).T.astype(BF)
-        return carry
-
-    half_cols, group = dq.shape[3], heads // 2
-
-    def one_half(half, carry):
-        lax.fori_loop(half * group, (half + 1) * group, attend, 0)
-        cols = pl.ds(pl.multiple_of(half * half_cols, 128), half_cols)
-        block = dqkv.at[:, cols]
-        for p in range(3):
-            for i in range(group):
-                lo = (p * group + i) * HD
-                block[:, lo : lo + HD] = dqh[p * heads + half * group + i, :, 0:HD]
-        block[:, 3 * group * HD :] = jnp.zeros((PADS, half_cols - 3 * group * HD), BF)
-
-        def qkv_grad(j, c):
-            dq[half, j] = tn(f1b[j], block[...]).astype(BF)
-            return c
-
-        lax.fori_loop(0, 4, qkv_grad, 0)
-
-        @pl.when(half == 0)
+    def attention(qh, oh, lse, dh, dqh):
+        inner = [moves.start(a, b) for a, b in ((qh_h, qh), (oh_h, oh), (lse_h, lse))]
+        ring_d.third()
+        dh[...] = jnp.zeros_like(dh)
+        for c in got:
+            c.wait()
+        got_o()
+        dqkv[:, 0:hw] = nn(dbr[...], gov[...]).astype(BF)
+        for h in range(heads):
+            dh[h, :, 0:HD] = dqkv[:, h * HD : (h + 1) * HD]
+
+        def out_grad(j, carry):
+            do[j] = tn(hflat[...], dbrb[j]).astype(BF)
+            return carry
+
+        lax.fori_loop(0, 4, out_grad, 0)
+        ring_d.fourth()
+        if summed:
+            sums[0].start()
+        for c in more + inner:
+            c.wait()
+        keymask = jnp.where(lax.broadcasted_iota(jnp.int32, (PADS, 1), 0) < SEQ, 0.0, -1e30)
+        ones = jnp.ones((8, 128), F32)
+
+        def attend(h, carry):
+            q, kk, v, g = qh[h], qh[heads + h], qh[2 * heads + h], dh[h]
+            p = jnp.exp(nt(kk, q) * HD ** (-0.5) + keymask - lse[pl.ds(h, 1), :])
+            delta = lax.dot_general(
+                ones, g.astype(F32) * oh[h].astype(F32), (((1,), (1,)), ((), ())),
+                precision=lax.Precision.HIGHEST, preferred_element_type=F32,
+            )[0:1]
+            ds = (p * (nt(v, g) - delta)).astype(BF)
+            dqh[2 * heads + h] = nn(p.astype(BF), g).astype(BF)
+            dqh[heads + h] = (nn(ds, q) * HD ** (-0.5)).astype(BF)
+            dqh[h] = (tn(kk, ds) * HD ** (-0.5)).T.astype(BF)
+            return carry
+
+        half_cols, group = dq.shape[3], heads // 2
+
+        def one_half(half, carry):
+            lax.fori_loop(half * group, (half + 1) * group, attend, 0)
+            cols = pl.ds(pl.multiple_of(half * half_cols, 128), half_cols)
+            block = dqkv.at[:, cols]
+            for p in range(3):
+                for i in range(group):
+                    lo = (p * group + i) * HD
+                    block[:, lo : lo + HD] = dqh[p * heads + half * group + i, :, 0:HD]
+            block[:, 3 * group * HD :] = jnp.zeros((PADS, half_cols - 3 * group * HD), BF)
+
+            def qkv_grad(j, c):
+                dq[half, j] = tn(f1b[j], block[...]).astype(BF)
+                return c
+
+            lax.fori_loop(0, 4, qkv_grad, 0)
+
+            @pl.when(half == 0)
+            def _():
+                ring_u.second()
+                ring_o.first()
+                ring_a.first()
+
+            return carry
+
+        lax.fori_loop(0, 2, one_half, 0)
+
+    pl.run_scoped(
+        attention,
+        pltpu.VMEM(qh_h.shape, BF), pltpu.VMEM(oh_h.shape, BF), pltpu.VMEM(lse_h.shape, F32),
+        pltpu.VMEM((heads,) + qh_h.shape[1:], BF), pltpu.VMEM(qh_h.shape, BF),
+    )
+    ring_b.first()
+
+    def ending(gqv, ps, home):
+        got_q = load_weight(wq, gq, gqv, lsem.at[1], k, is_a)
+        ring_d.home_sent()
+        ring_u.third()
+        ring_u.fourth()
+        if summed:
+            sums[1].start()
+        ring_o.second()
+        got_q()
+
+        def first_grad(c, n):
+            rows = pl.ds(c, n)
+            ps[:, rows] = nt(dqkv[...], gqv[rows, :]).astype(BF)
+
+        chunks(ps.shape[1], 384, first_grad)
+        exchange = remote(ps, pr, es, er, at(x, 1 - k, y))
+        exchange.start()
+        ring_a.second()
+
+        def bias_grad(c, n):
+            cols = pl.ds(c, n)
+            colv[0:1, cols] = jnp.sum(dqkv[:, cols].astype(F32), axis=0, keepdims=True)
+
+        chunks(dqkv.shape[1], 128, bias_grad)
+        colv[1:2, :] = dbu[...]
+        exchange.wait_recv()
+        exchange.wait_send()
+        g1 = xb[SEQ - 1 : PADS, :].astype(F32)[1:2]
+        acc[...] = jnp.zeros_like(acc)
+
+        def norm1(r, n):
+            rows = pl.ds(r, n)
+            back, normed, incoming = norm_back_rows(xb[rows, :].astype(F32), ps[rows, :], pr[rows, :], g1)
+            ps[rows, :] = (dbr[rows, :].astype(F32) + back).astype(BF)
+            fold(acc, 0, incoming * normed)
+            fold(acc, 1, incoming)
+
+        chunks(PADS, 128, norm1)
+        gain, shift = (jnp.sum(acc[i], axis=0, keepdims=True) for i in range(2))
+        rows6 = jnp.concatenate(
+            [gain, vec2[0:1], shift, vec2[1:2], vec2[2:3], vec2[3:4], jnp.zeros((2, 4 * width), F32)], axis=0
+        )
+        for j in range(4):
+            rowb[j] = rows6[:, j * width : (j + 1) * width]
+        for c in row_sends + col_sends:
+            c.start()
+        pl.when(is_b)(col_extra.start)
+        low = k == 0
+        for i in range(2):
+            lo = 2 * i * width
+            home[i] = jnp.where(low, ps[:, lo : lo + width], ps[:, lo + width : lo + 2 * width])
+        mine = pltpu.make_async_copy(home.at[0], gin.at[x], cs)
+        mine.start()
+        away = remote(home.at[1], gin.at[x], hs, hr, at(1 - x, k, y))
+        away.start()
+        ring_b.second()
+        ring_o.third()
+        ring_o.fourth()
+        if summed:
+            sums[0].finish()
+            sums[2].start()
+        ring_a.third()
+        ring_a.fourth()
+        if summed:
+            sums[3].start()
+        for c in row_sends:
+            c.wait_recv()
+        for i in range(1, 4):
+            remote(colv, cr.at[i], vs.at[3], vr.at[3 + i], at(x, 1 - k, k)).wait_recv()
+        pl.when(is_b)(lambda: remote(colv, cr.at[0], vs.at[3], vr.at[3], at(x, 1 - k, k)).wait_recv())
+        rsum[...] = rowb[k] + rr[0] + rr[1] + rr[2]
+
+        @pl.when(is_a)
         def _():
-            ring_u.second()
-            ring_a.first()
-            ring_d.third(settled=True)
-            ring_d.fourth()
-            if summed:
-                sums[0].start()
-
-        return carry
-
-    lax.fori_loop(0, 2, one_half, 0)
-    ring_b.first()
-    ring_o.second()
-    got_q()
-
-    def first_grad(c, n):
-        rows = pl.ds(c, n)
-        ps[:, rows] = nt(dqkv[...], gqv[rows, :]).astype(BF)
-
-    chunks(ps.shape[1], 384, first_grad)
-    exchange = remote(ps, pr, es, er, at(x, 1 - k, y))
-    exchange.start()
-    ring_d.home_sent()
-    ring_u.third()
-    ring_u.fourth()
-    ring_a.second()
-    if summed:
-        sums[1].start()
-
-    def bias_grad(c, n):
-        cols = pl.ds(c, n)
-        colv[0:1, cols] = jnp.sum(dqkv[:, cols].astype(F32), axis=0, keepdims=True)
-
-    chunks(dqkv.shape[1], 128, bias_grad)
-    colv[1:2, :] = dbu[...]
-    exchange.wait_recv()
-    exchange.wait_send()
-    g1 = xb[SEQ - 1 : PADS, :].astype(F32)[1:2]
-    acc[...] = jnp.zeros_like(acc)
-
-    def norm1(r, n):
-        rows = pl.ds(r, n)
-        back, normed, incoming = norm_back_rows(xb[rows, :].astype(F32), ps[rows, :], pr[rows, :], g1)
-        ps[rows, :] = (dbr[rows, :].astype(F32) + back).astype(BF)
-        fold(acc, 0, incoming * normed)
-        fold(acc, 1, incoming)
-
-    chunks(PADS, 128, norm1)
-    gain, shift = (jnp.sum(acc[i], axis=0, keepdims=True) for i in range(2))
-    rows6 = jnp.concatenate(
-        [gain, vec2[0:1], shift, vec2[1:2], vec2[2:3], vec2[3:4], jnp.zeros((2, 4 * width), F32)], axis=0
-    )
-    for j in range(4):
-        rowb[j] = rows6[:, j * width : (j + 1) * width]
-    for c in row_sends + col_sends:
-        c.start()
-    pl.when(is_b)(col_extra.start)
-    low = k == 0
-    for i in range(2):
-        lo = 2 * i * width
-        home[i] = jnp.where(low, ps[:, lo : lo + width], ps[:, lo + width : lo + 2 * width])
-    mine = pltpu.make_async_copy(home.at[0], gin.at[x], cs)
-    mine.start()
-    away = remote(home.at[1], gin.at[x], hs, hr, at(1 - x, k, y))
-    away.start()
-    ring_b.second()
-    ring_o.third()
-    ring_o.fourth()
-    if summed:
-        sums[0].finish()
-        sums[2].start()
-    ring_a.third()
-    ring_a.fourth()
-    if summed:
-        sums[3].start()
-    for c in row_sends:
-        c.wait_recv()
-    for i in range(1, 4):
-        remote(colv, cr.at[i], vs.at[3], vr.at[3 + i], at(x, 1 - k, k)).wait_recv()
-    pl.when(is_b)(lambda: remote(colv, cr.at[0], vs.at[3], vr.at[3], at(x, 1 - k, k)).wait_recv())
-    rsum[...] = rowb[k] + rr[0] + rr[1] + rr[2]
-
-    @pl.when(is_a)
-    def _():
-        csum[...] = colv[...] + cr[1] + cr[2] + cr[3]
-
-    @pl.when(is_b)
-    def _():
-        csum[...] = cr[0] + cr[1] + cr[2] + cr[3]
-
-    for c in dp_sends:
-        c.start()
-    ring_b.third()
-    ring_b.fourth()
-    if summed:
-        sums[4].start()
-        sums[1].finish()
-    mine.wait()
-    remote(home.at[1], gin.at[1 - x], hs, hr, at(1 - x, k, y)).wait_recv()
-    away.wait_send()
-    for ring in (ring_u, ring_o, ring_a, ring_b):
-        ring.close()
-    for c in row_sends + col_sends:
-        c.wait_send()
-    pl.when(is_b)(col_extra.wait_send)
-    for c in dp_sends:
-        c.wait_recv()
-        c.wait_send()
-    rowt[...] = rsum[...] + sum(rz[o] for o in range(size - 1))
-    colt[...] = csum[...] + sum(cz[o] for o in range(size - 1))
-    if summed:
-        for total in sums[2:]:
-            total.finish()
-        for total in sums:
-            total.close()
-
-
-def backward(parts, du, dd, rd, go, wo, gq, wq, xb, f1b, hflat, qh, oh, lse, dbr, dbrb, vec2, dbu):
-    width, ff = du.shape[1:]
-    hw, nq = wo.shape[1], wq.shape[1]
-    full, heads = 4 * width, hw // HD
-    anyspec = pl.BlockSpec(memory_space=pl.ANY)
-    vspec = pl.BlockSpec(memory_space=pltpu.VMEM)
-    shape = jax.ShapeDtypeStruct
-    dma = pltpu.SemaphoreType.DMA
+            csum[...] = colv[...] + cr[1] + cr[2] + cr[3]
+
+        @pl.when(is_b)
+        def _():
+            csum[...] = cr[0] + cr[1] + cr[2] + cr[3]
+
+        for c in dp_sends:
+            c.start()
+        ring_b.third()
+        ring_b.fourth()
+        if summed:
+            sums[4].start()
+            sums[1].finish()
+        mine.wait()
+        remote(home.at[1], gin.at[1 - x], hs, hr, at(1 - x, k, y)).wait_recv()
+        away.wait_send()
+        for ring in (ring_u, ring_o, ring_a, ring_b):
+            ring.close()
+        for c in row_sends + col_sends:
+            c.wait_send()
+        pl.when(is_b)(col_extra.wait_send)
+        for c in dp_sends:
+            c.wait_recv()
+            c.wait_send()
+        rowt[...] = rsum[...] + sum(rz[o] for o in range(size - 1))
+        colt[...] = csum[...] + sum(cz[o] for o in range(size - 1))
+        if summed:
+            for total in sums[2:]:
+                total.finish()
+            for total in sums:
+                total.close()
+
+        later()
+        ring_d.close(home=False)
+
+    pl.run_scoped(
+        ending, pltpu.VMEM((4 * width, wq.shape[1]), BF), pltpu.VMEM(pr.shape, BF), pltpu.VMEM((2, PADS, width), BF)
+    )
+
+
+def layer(parts, tok, cot, bias, wq, wo, wu, wd):
+    width, hw, ff, nq = tok.shape[2], wo.shape[1], wu.shape[1], wq.shape[1]
+    full, heads, nh = 4 * width, hw // HD, nq // 2
     others = max(parts - 1, 1)
     peers = lax.axis_size("dp") - 1
     piece, slab = width // parts, hw // parts
-    nh = nq // 2
-    outs = [
-        shape((parts, piece, ff), BF), shape((5, width, ff), BF), shape((parts, piece, ff), BF),
-        shape((5, hw, width), BF), shape((parts, slab, width), BF),
-        shape((5, width, nh), BF), shape((parts, piece, nh), BF), shape((5, width, nh), BF), shape((parts, piece, nh), BF),
-        shape((others, piece, ff), BF), shape((others, piece, ff), BF), shape((others, slab, width), BF),
-        shape((others, piece, nh), BF), shape((others, piece, nh), BF), shape((2, PADS, width), BF),
-        *(
-            shape(d if parts > 1 else (8, 128), F32)
-            for d in ((piece, ff), (piece, ff), (slab, width), (piece, nh), (piece, nh))
-        ),
-        shape((8, width), F32), shape((2, ff), F32),
-    ]
-    return pl.pallas_call(
-        backward_kernel,
-        out_shape=outs,
-        in_specs=[anyspec] * 17,
-        out_specs=[anyspec] * 15 + [vspec] * 7,
-        scratch_shapes=[pltpu.VMEM(a.shape, a.dtype) for a in (xb, f1b, hflat, qh, oh, lse, dbr, dbrb, vec2, dbu)]
-        + [
-            pltpu.VMEM((2, 8, full), F32), pltpu.VMEM((full, hw), BF), pltpu.VMEM((full, nq), BF),
-            pltpu.VMEM((heads, PADS, 128), BF), pltpu.VMEM((3 * heads, PADS, 128), BF), pltpu.VMEM((PADS, nq), BF),
-            pltpu.VMEM((PADS, full), BF), pltpu.VMEM((PADS, full), BF),
-            pltpu.VMEM((4, hw, width), BF), pltpu.VMEM((2, 4, width, nh), BF), pltpu.VMEM((2, PADS, width), BF),
-        ]
-        + scatter_scratch(width, ff, parts) + scatter_scratch(hw, width, parts)
-        + scatter_scratch(width, nh, parts) + scatter_scratch(width, nh, parts) + [dma((4,)), dma((6,))]
-        + [
-            pltpu.VMEM((4, 8, width), F32), pltpu.VMEM((2, ff), F32), pltpu.VMEM((3, 8, width), F32), pltpu.VMEM((4, 2, ff), F32),
-            pltpu.VMEM((8, width), F32), pltpu.VMEM((2, ff), F32), pltpu.VMEM((peers, 8, width), F32), pltpu.VMEM((peers, 2, ff), F32),
-        ]
-        + [dma((2, 4)), dma((5, others)), dma((5, others)), dma((5, others + 1)), dma(()), dma(()), dma(()), dma(()), dma(()),
-           dma((7,)), dma((7,)), dma((2, peers)), dma((2, peers)), dma((10,))],
-        compiler_params=pltpu.CompilerParams(collective_id=2, has_side_effects=True, vmem_limit_bytes=VMEM_CAP),
-        name="backward",
-    )(du, dd, rd, go, wo, gq, wq, xb, f1b, hflat, qh, oh, lse, dbr, dbrb, vec2, dbu)
+    low = lambda *d: (d, BF)
+    wide = lambda *d: (d, F32)
+    tall, rows4 = low(PADS, full), low(4, PADS, width)
+    hbm = dict(
+        gq=low(4, width, nq), go=low(4, width, hw), gu=low(4, width, ff), gd=low(4, width, ff),
+        xb=tall, dyb=tall, f1b=rows4, qh=low(3 * heads, PADS, 128), oh=low(heads, PADS, 128), hflat=low(PADS, hw),
+        lse=wide(heads, PADS), residual=wide(PADS, full), f2b=rows4, hidden=low(PADS, ff), slope=low(PADS, ff),
+        dd=low(4, width, ff), tbuf=rows4, cbuf=rows4, rd=low(5, width, ff), outb=low(2, PADS, width),
+        du=low(4, width, ff), dbr=tall, dbrb=rows4, rowv=wide(8, full), dbu=wide(1, ff),
+        zsd=low(parts, piece, ff), ru=low(5, width, ff), zsu=low(parts, piece, ff),
+        ro=low(5, hw, width), zso=low(parts, slab, width),
+        ra=low(5, width, nh), zsa=low(parts, piece, nh), rb=low(5, width, nh), zsb=low(parts, piece, nh),
+        zrd=low(others, piece, ff), zru=low(others, piece, ff), zro=low(others, slab, width),
+        zra=low(others, piece, nh), zrb=low(others, piece, nh), gin=low(2, PADS, width),
+    )
+    small = [(piece, ff), (piece, ff), (slab, width), (piece, nh), (piece, nh)]
+    vmem_out = dict(
+        zip(("td", "tu", "to", "ta", "tb"), [wide(*d) if parts > 1 else wide(8, 128) for d in small]),
+        rowt=wide(8, width), colt=wide(2, ff),
+    )
+    kept = dict(
+        bv=low(*bias.shape), precv_f=tall, precv_m=tall, orecv=low(2, PADS, width), theirs=low(2, PADS, width),
+        pr=tall, sbd=low(width, ff), rowb=wide(4, 8, width), colv=wide(2, ff), rr=wide(3, 8, width), cr=wide(4, 2, ff),
+        rsum=wide(8, width), csum=wide(2, ff), rz=wide(peers, 8, width), cz=wide(peers, 2, ff),
+    )
+    sems = dict(
+        ssem=(8,), rsem=(8,), csem=(3,), lsem=(4,), wsend=(4, 4), wrecv=(4, 4), msem_f=(12,),
+        ssd=(4,), rsd=(6,), lsd=(6,), lsem_m=(2, 4), ps_m=(3,), pr_m=(3,), cs_m=(), msem_m=(11,),
+        ssu=(4,), rsu=(6,), lsu=(6,), sso=(4,), rso=(6,), lso=(6,), ssa=(4,), rsa=(6,), lsa=(6,), ssb=(4,), rsb=(6,), lsb=(6,),
+        lsem_b=(2, 4), zss=(5, others), zrs=(5, others), zls=(5, others + 1), es=(), er=(), hs=(), hr=(), cs=(),
+        vs=(7,), vr=(7,), ws=(2, peers), wr=(2, peers), msem_b=(10,),
+    )
+    names = ["tok", "cot", "bias", "wq", "wo", "wu", "wd", *hbm, *vmem_out, *kept, *sems]
+
+    def scoped(fn, shapes):
+        pl.run_scoped(fn, *[pltpu.VMEM(d, t) for d, t in shapes])
+
+    def kernel(*refs):
+        r = types.SimpleNamespace(**dict(zip(names, refs)))
+        x, k, y = spot = place()
+        size, me = lax.axis_size("dp"), lax.axis_index("dp")
+        plane = [at(1 - x, k, y), at(x, k, 1 - y), at(1 - x, k, 1 - y), at(x, 1 - k, y)]
+        plane += [at(1 - x, 1 - k, y), at(x, 1 - k, 1 - y), at(1 - x, 1 - k, 1 - y)]
+        greet(plane + [{"dp": lax.rem(me + o, size)} for o in range(1, size)])
+
+        def first_ring():
+            Scatter(r.dd, r.rd, None, None, r.sbd, None, r.ssd, r.rsd, r.lsd, spot).first()
+
+        def second_ring():
+            Scatter(r.du, r.ru, None, None, None, None, r.ssu, r.rsu, r.lsu, spot).first()
+
+        scoped(
+            lambda *v: forward_phase(
+                r.tok, r.cot, r.bias, r.wq, r.wo, r.wu, r.wd,
+                r.gq, r.go, r.gu, r.gd, r.xb, r.dyb, r.f1b, r.qh, r.oh, r.hflat, r.lse, r.residual, r.f2b,
+                r.hidden, r.slope, r.dd, r.tbuf, r.cbuf, r.bv, r.precv_f,
+                r.ssem, r.rsem, r.csem, r.lsem, r.wsend, r.wrecv, r.msem_f, spot, first_ring, *v,
+            ),
+            [hbm[n] for n in ("xb", "dyb", "f1b", "qh", "oh", "hflat", "lse", "residual", "f2b", "hidden", "slope", "dd")]
+            + [rows4, low(full, nq), low(full, hw), low(full, ff), tall, tall],
+        )
+
+        def later():
+            far = at(1 - x, k, y)
+            pltpu.make_async_copy(r.theirs.at[0], r.outb.at[x], r.cs_m).wait()
+            remote(r.theirs.at[1], r.outb.at[1 - x], r.ps_m.at[2], r.pr_m.at[2], far).wait_recv()
+            remote(r.theirs.at[1], r.outb.at[x], r.ps_m.at[2], r.pr_m.at[2], far).wait_send()
+
+        scoped(
+            lambda *v: middle_phase(
+                r.dd, r.gd, r.wd, r.gu, r.wu, r.xb, r.dyb, r.residual, r.f2b, r.hidden, r.slope,
+                r.rd, r.outb, r.du, r.dbr, r.dbrb, r.rowv, r.dbu, r.precv_m, r.orecv, r.theirs, r.sbd,
+                r.ssd, r.rsd, r.lsd, r.lsem_m, r.ps_m, r.pr_m, r.cs_m, r.msem_m, spot, second_ring, *v,
+            ),
+            [hbm[n] for n in ("xb", "dyb", "residual", "f2b", "hidden", "slope", "du", "dbr", "dbrb", "rowv", "dbu")]
+            + [wide(4, 8, full), tall, low(full, ff), low(full, ff), low(PADS, ff), low(2, PADS, width), wide(PADS, full),
+               low(3, width, ff)],
+        )
+        scoped(
+            lambda *v: backward_phase(
+                r.du, r.dd, r.rd, r.go, r.wo, r.gq, r.wq, r.xb, r.f1b, r.hflat, r.qh, r.oh, r.lse, r.dbr, r.dbrb, r.rowv, r.dbu,
+                r.zsd, r.ru, r.zsu, r.ro, r.zso, r.ra, r.zsa, r.rb, r.zsb, r.zrd, r.zru, r.zro, r.zra, r.zrb, r.gin,
+                r.td, r.tu, r.to, r.ta, r.tb, r.rowt, r.colt,
+                r.pr, r.sbd, r.rowb, r.colv, r.rr, r.cr, r.rsum, r.csum, r.rz, r.cz,
+                r.ssu, r.rsu, r.lsu, r.sso, r.rso, r.lso, r.ssa, r.rsa, r.lsa, r.ssb, r.rsb, r.lsb, r.ssd, r.rsd,
+                r.lsem_b, r.zss, r.zrs, r.zls, r.es, r.er, r.hs, r.hr, r.cs, r.vs, r.vr, r.ws, r.wr, r.msem_b,
+                spot, later, *v,
+            ),
+            [hbm[n] for n in ("xb", "f1b", "hflat", "dbr", "dbrb", "rowv", "dbu")]
+            + [wide(2, 8, full), low(full, hw), low(PADS, nq), low(4, hw, width), low(2, 4, width, nh)]
+            + [low(3, width, ff), low(width, ff), low(2, parts, piece, ff)]
+            + [low(3, hw, width), low(hw, width), low(2, parts, slab, width)]
+            + [low(3, width, nh), low(width, nh), low(2, parts, piece, nh), low(width, nh), low(2, parts, piece, nh)],
+        )
+
+    anyspec = pl.BlockSpec(memory_space=pl.ANY)
+    outs = pl.pallas_call(
+        kernel,
+        out_shape=[jax.ShapeDtypeStruct(*v) for v in (*hbm.values(), *vmem_out.values())],
+        in_specs=[anyspec] * 7,
+        out_specs=[anyspec] * len(hbm) + [pl.BlockSpec(memory_space=pltpu.VMEM)] * len(vmem_out),
+        scratch_shapes=[pltpu.VMEM(*v) for v in kept.values()] + [pltpu.SemaphoreType.DMA(v) for v in sems.values()],
+        compiler_params=pltpu.CompilerParams(collective_id=0, has_side_effects=True, vmem_limit_bytes=VMEM_CAP),
+        name="layer",
+    )(tok, cot, bias, wq, wo, wu, wd)
+    return types.SimpleNamespace(**dict(zip((*hbm, *vmem_out), outs)))
 
 
 def shards(tokens, ln_gain, ln_bias, w_qkv, b_qv, w_out, b_out, w_up, b_up, w_down, b_down, cotangent):
@@ -993,23 +993,18 @@
         [w_qkv[:, p, i * hh : (i + 1) * hh] if p < 3 else side for i in range(2) for p in range(4)], axis=1
     )
     wot, wdt = w_out.T, w_down.T
-    gq, go, gu, gd, xb, dy, f1b, qh, oh, hflat, lse, residual, f2b, hidden, slope, dd = forward(
-        tok2, cot2, bias, qblock, wot, w_up, wdt
-    )
     dp_size = lax.axis_size("dp")
     parts = dp_size if width % dp_size == 0 and (width // dp_size) % 8 == 0 else 1
-    rd, outb, du, dbr, dbrb, vec2, dbu = middle(dd, gd, wdt, gu, w_up, xb, dy, residual, f2b, hidden, slope)
-    output = jnp.concatenate([outb[i, :SEQ] for i in range(images)])
-    back = backward(parts, du, dd, rd, go, wot, gq, qblock, xb, f1b, hflat, qh, oh, lse, dbr, dbrb, vec2, dbu)
-    zsd, _, zsu, _, zso, _, zsa, _, zsb = back[:9]
-    gin, td, tu, to, ta, tb, rowt, colt = back[14:]
-    input_grad = jnp.concatenate([gin[i, :SEQ] for i in range(images)])
+    r = layer(parts, tok2, cot2, bias, qblock, wot, w_up, wdt)
+    output = jnp.concatenate([r.outb[i, :SEQ] for i in range(images)])
+    input_grad = jnp.concatenate([r.gin[i, :SEQ] for i in range(images)])
+    td, tu, to, ta, tb, rowt, colt = r.td, r.tu, r.to, r.ta, r.tb, r.rowt, r.colt
     if parts == 1:
 
         def over_dp(a):
             return lax.psum_scatter(a[0], "dp", scatter_dimension=0, tiled=True).astype(F32)
 
-        td, tu, to, ta, tb = (over_dp(a) for a in (zsd, zsu, zso, zsa, zsb))
+        td, tu, to, ta, tb = (over_dp(a) for a in (r.zsd, r.zsu, r.zso, r.zsa, r.zsb))
 
     return (
         output,

time: 385 us -> 369 us (0.958)
  Pallas kernels: 354 us -> 339 us
    pallas_call x3 -> x1, Pallas kernels: 354 us -> 339 us  [layer(): pl.pallas_call(kernel, out_shape=[jax.ShapeDtypeStruct(*v) for v in (*hbm...]
    unnamed x36 -> x38, local copies, waits for them, and re-layouts: 8.42 us -> 8.42 us
where the time goes in v1:
time: 369 us; the launch traced here: 366 us
  Pallas kernels  339 us (92%)
  local copies, waits for them, and re-layouts  21.1 us (6%)
  other arithmetic  4.9 us (1%)
    pallas_call x1, Pallas kernels, layer(): pl.pallas_call(kernel, out_shape=[jax.ShapeDtypeStruct(*v) for v in (*hbm...  339 us
    unnamed x38, local copies, waits for them, and re-layouts  8.42 us

profile of v1, /device:TPU:0, one launch (start us, length us, event | category | flops | bytes accessed | tf_op | source)
XLA Modules:
  0.0 365.9 jit_solution(13906275637824165983)
XLA Ops:
  0.6 0.0 copy-start.2
  0.7 0.1 pad.16.clone
  0.7 0.7 broadcast_in_dim.31
  1.5 0.7 broadcast_in_dim.32
  2.2 0.9 slice_reduce_fusion.7
  3.1 0.1 concatenate.43
  3.2 0.7 broadcast_in_dim.38
  3.9 0.7 maximum_maximum_fusion.refs_2_
  4.6 1.1 slice.110
  5.7 0.3 copy.41
  6.0 0.0 copy-done.2
  6.0 0.2 slice.111
  6.2 0.3 copy.42
  6.5 0.3 pad_bitcast_fusion
  6.8 0.0 copy-start.3
  6.8 1.2 pad_maximum_fusion.1.refs_1_
  8.0 0.2 fusion
  8.2 0.3 copy.39
  8.5 0.2 copy-done.11
  8.7 0.0 copy-done.12
  8.7 0.9 concatenate.39
  9.6 0.3 copy.40
  9.9 0.0 copy-start
  9.9 0.9 concatenate.40
  10.8 1.2 pad_maximum_fusion.refs_0_
  12.0 0.3 slice_bitcast_fusion.4
  12.4 2.0 concatenate.45.refs_3_
  14.4 339.0 %layer.1 = (bf16[4,288,1792]{2,1,0:T(8,128)(2,1)}, bf16[4,288,576]{2,1,0:T(8,128)(2,1)}, bf16[4,288,2152]{2,1,0:T(8,128)(2,1)}, bf16[4,288,2152]{2,1,0:T(8,128)(...) custom-call(bf16[2,736,288]{2,1,0:T(8,128)(2,1)} %pad_maximum_fusion, ...), custom_call_target="tpu_custom_call" | custom-call | tf_op jit(solution)/shard_map/layer/pallas_call | solution.py:957
  353.4 1.3 slice_bitcast_fusion.3
  354.8 0.2 pad_maximum_fusion.2
  355.0 1.9 copy.36
  356.9 0.6 slice_reduce_fusion.1
  357.5 0.6 fusion.1
  358.1 0.1 slice_reduce_fusion.6
  358.2 0.6 slice_reduce_fusion
  358.8 0.1 pad_maximum_fusion.6
  358.9 0.1 pad_maximum_fusion.7
  359.0 0.6 pad_maximum_fusion.5
  359.6 0.2 reshape.34
  359.8 0.2 reshape.35
  360.1 0.3 pad_maximum_fusion.4
  360.4 0.8 copy.38
  361.2 0.1 slice_bitcast_fusion.1
  361.4 0.2 pad_maximum_fusion.3
  361.6 1.9 copy.37
  363.5 0.7 copy.46
  364.2 0.8 copy.47
  365.0 0.8 copy.48
  (31 shorter events, 0.1 us)
Async XLA Ops:
  0.6 5.4 %copy-start.2 = (bf16[1458,288]{0,1:T(8,128)(2,1)S(1)}, bf16[1458,288]{0,1:T(8,128)(2,1)}, u32[]{:S(2)}) copy-start(bf16[1458,288]{0,1:T(8,128)(2,1)} %param.23) | copy-start | bytes 2519428
  4.6 1.9 copy-start.13
  6.8 1.2 copy-start.3
  8.0 0.7 copy-start.11
  8.0 0.7 copy-start.12
  9.9 2.2 copy-start
  354.7 2.2 copy-start.10
  354.7 3.3 copy-start.9
  354.7 4.8 %copy-start.7 = (f32[72,896]{1,0:T(8,128)S(1)}, f32[72,896]{1,0:T(8,128)}, u32[]{:S(2)}) copy-start(f32[72,896]{1,0:T(8,128)} %get-tuple-element.24) | copy-start | bytes 774148
  355.0 4.9 %copy-start.6 = (f32[72,896]{1,0:T(8,128)S(1)}, f32[72,896]{1,0:T(8,128)}, u32[]{:S(2)}) copy-start(f32[72,896]{1,0:T(8,128)} %get-tuple-element.25) | copy-start | bytes 774148
  359.8 1.4 copy-start.1
  361.4 2.2 copy-start.8
  361.6 2.6 copy-start.5
  361.6 3.4 copy-start.4

commit v2 on v1

--- a/solution.py
+++ b/solution.py
@@ -99,6 +99,7 @@
     width = tok.shape[2]
     blocks, wholes = (wq, wo, wu, wd), (gq, go, gu, gd)
     out = Moves(msem)
+    over_y = (1,)
 
     def own_sends(w):
         b, g = blocks[w], wholes[w]
@@ -118,6 +119,7 @@
         return (
             remote(g.at[2], g.at[2], wsend.at[w, 3], wrecv.at[w, 2], at(x, k, 1 - y)),
             remote(g.at[1], g.at[3], wsend.at[w, 3], wrecv.at[w, 3], at(1 - x, k, y)),
+            remote(g.at[3], g.at[3], wsend.at[w, 2], wrecv.at[w, 3], at(x, k, 1 - y)),
         )
 
     def both(fa, fb):
@@ -132,30 +134,39 @@
         remote(blocks[w], wholes[w].at[j], wsend.at[w, 0], wrecv.at[w, j], at(x, 1 - k, y)).wait_recv()
 
     def start_relay(w):
-        ra, rb = relays(w)
+        ra, rb, rc = relays(w)
 
         def fa():
             arrived(w, 2)
             ra.start()
+            if w in over_y:
+                arrived(w, 3)
+                rc.start()
 
         def fb():
             arrived(w, 1)
             rb.start()
 
-        both(fa, fb)
+        pl.when(is_a)(fa)
+        if w not in over_y:
+            pl.when(is_b)(fb)
 
     def wait_rest(w):
         pl.when(is_b | (k == 1))(lambda: arrived(w, 0))
         pl.when(is_a & (k == 0))(lambda: arrived(w, 1))
         pl.when(is_b)(lambda: arrived(w, 2))
-        arrived(w, 3)
+        if w in over_y:
+            pl.when(is_b)(lambda: (arrived(w, 1), arrived(w, 3)) and None)
+        else:
+            arrived(w, 3)
 
     def finish_sends(w):
         a, b = own_sends(w)
-        ra, rb = relays(w)
+        ra, rb, rc = relays(w)
+        a, b = (a + [ra, rc], b) if w in over_y else (a + [ra], b + [rb])
         both(
-            lambda: [c.wait_send() for c in a + [ra]] and None,
-            lambda: [c.wait_send() for c in b + [rb]] and None,
+            lambda: [c.wait_send() for c in a] and None,
+            lambda: [c.wait_send() for c in b] and None,
         )
 
     def load(w, dst):
@@ -970,24 +981,28 @@
     width = tokens.shape[1]
     hw = b_qv.shape[1]
 
-    extra = jnp.concatenate(
-        [ln_gain, ln_bias, b_out[None], b_down[None], jnp.zeros((1, width), BF)], axis=0
-    )
     images = tokens.shape[0] // SEQ
-    blank = jnp.zeros((PADS - SEQ, width), BF)
-
-    def with_rows(a, tail):
-        return jnp.stack([jnp.concatenate([a[i * SEQ : (i + 1) * SEQ], tail]) for i in range(images)])
-
-    tok2, cot2 = with_rows(tokens, extra), with_rows(cotangent, blank)
     ff = b_up.shape[0]
     nq, hh = padded(hw), hw // 2
+
+    def put(a, shape, *spot):
+        a = a.reshape((1,) * (len(shape) - a.ndim) + a.shape)
+        return jnp.pad(a, [(lo, n - m - lo) for lo, n, m in zip(spot, shape, a.shape)])
+
+    wide = (images, PADS, width)
+    vectors = sum(
+        put(v, (PADS, width), SEQ + i, 0) for i, v in enumerate((ln_gain[0], ln_gain[1], ln_bias[0], ln_bias[1], b_out, b_down))
+    )
+
+    def halves(a):
+        return sum(put(a[i * SEQ : (i + 1) * SEQ], wide, i, 0, 0) for i in range(images))
+
+    tok2, cot2 = halves(tokens) + vectors[None], halves(cotangent)
+    bias = put(b_up, (16, ff), 1, 0)
+    for i in range(2):
+        for p in (0, 2):
+            bias += put(b_qv[p // 2, i * hh : (i + 1) * hh], (16, ff), 0, i * nq // 2 + p * hh)
     gap = jnp.zeros((nq // 2 - 3 * hh,), BF)
-    nil = jnp.zeros((hh,), BF)
-    bqkv = jnp.concatenate(
-        [b_qv[0, :hh], nil, b_qv[1, :hh], gap, b_qv[0, hh:], nil, b_qv[1, hh:], gap, jnp.zeros((ff - nq,), BF)]
-    )
-    bias = jnp.concatenate([bqkv[None], b_up[None], jnp.zeros((14, ff), BF)])
     side = jnp.zeros((width, gap.shape[0]), BF)
     qblock = jnp.concatenate(
         [w_qkv[:, p, i * hh : (i + 1) * hh] if p < 3 else side for i in range(2) for p in range(4)], axis=1

time: 369 us -> 365 us (0.989)
    unnamed x38 -> x30, local copies, waits for them, and re-layouts: 8.42 us -> 8.33 us
where the time goes in v2:
time: 365 us; the launch traced here: 363 us
  Pallas kernels  337 us (92%)
  local copies, waits for them, and re-layouts  20 us (5%)
  other arithmetic  4.65 us (1%)
    pallas_call x1, Pallas kernels, layer(): pl.pallas_call(kernel, out_shape=[jax.ShapeDtypeStruct(*v) for v in (*hbm...  337 us
    unnamed x30, local copies, waits for them, and re-layouts  8.33 us

profile of v2, /device:TPU:0, one launch (start us, length us, event | category | flops | bytes accessed | tf_op | source)
XLA Modules:
  0.0 362.7 jit_solution(5942288338970872452)
XLA Ops:
  0.6 0.7 reshape.58
  1.3 0.7 reshape.59
  2.0 0.8 fusion.4
  2.8 0.9 fusion.3
  3.7 0.7 reshape.62
  4.4 0.7 pad_add_fusion.2.refs_2_
  5.1 0.1 pad_add_fusion.1
  5.2 1.4 fusion.1
  6.5 0.3 copy.39
  6.8 0.3 copy.40
  7.1 0.0 copy-start.2
  7.1 1.3 add_add_fusion.refs_0_
  8.4 0.0 copy-done.2
  8.4 0.2 fusion
  8.6 0.3 copy.41
  8.9 0.0 copy-start
  8.9 0.3 copy.42
  9.2 1.1 pad_add_fusion.refs_1_
  10.4 0.0 copy-done
  10.4 0.3 slice_bitcast_fusion.4
  10.7 2.2 concatenate.18.refs_3_
  12.9 337.3 %layer.1 = (bf16[4,288,1792]{2,1,0:T(8,128)(2,1)}, bf16[4,288,576]{2,1,0:T(8,128)(2,1)}, bf16[4,288,2152]{2,1,0:T(8,128)(2,1)}, bf16[4,288,2152]{2,1,0:T(8,128)(...) custom-call(bf16[2,736,288]{2,1,0:T(8,128)(2,1)} %add_add_fusion.ref, ...), custom_call_target="tpu_custom_call" | custom-call | tf_op jit(solution)/shard_map/layer/pallas_call | solution.py:968
  350.1 1.3 slice_bitcast_fusion.3
  351.5 0.2 pad_maximum_fusion
  351.7 1.9 copy.36
  353.6 0.6 slice_reduce_fusion.1
  354.2 0.6 fusion.2
  354.8 0.0 copy-done.8
  354.8 0.1 slice_reduce_fusion.6
  354.9 0.6 slice_reduce_fusion
  355.6 0.1 pad_maximum_fusion.4
  355.6 0.1 pad_maximum_fusion.5
  355.7 0.6 pad_maximum_fusion.3
  356.3 0.2 reshape.63
  356.6 0.0 copy-done.5
  356.6 0.2 reshape.64
  356.8 0.3 pad_maximum_fusion.2
  357.1 0.8 copy.38
  358.0 0.1 copy-done.1
  358.1 0.1 slice_bitcast_fusion.1
  358.2 0.2 pad_maximum_fusion.1
  358.4 1.9 copy.37
  360.4 0.0 copy-done.7
  360.4 0.7 copy.46
  361.1 0.0 copy-done.4
  361.1 0.8 copy.47
  361.9 0.0 copy-done.3
  361.9 0.8 copy.48
  (13 shorter events, 0.0 us)
Async XLA Ops:
  7.1 1.3 copy-start.2
  8.9 1.4 copy-start
  351.7 2.0 copy-start.9
  351.7 3.1 copy-start.8
  351.7 4.6 %copy-start.6 = (f32[72,896]{1,0:T(8,128)S(1)}, f32[72,896]{1,0:T(8,128)}, u32[]{:S(2)}) copy-start(f32[72,896]{1,0:T(8,128)} %get-tuple-element.24) | copy-start | bytes 774148
  351.7 4.9 %copy-start.5 = (f32[72,896]{1,0:T(8,128)S(1)}, f32[72,896]{1,0:T(8,128)}, u32[]{:S(2)}) copy-start(f32[72,896]{1,0:T(8,128)} %get-tuple-element.25) | copy-start | bytes 774148
  356.8 1.3 copy-start.1
  358.4 1.9 copy-start.7
  358.4 2.6 copy-start.4
  358.4 3.4 copy-start.3

commit v3 on v2

--- a/solution.py
+++ b/solution.py
@@ -561,8 +561,6 @@
         theirs[i] = (side(full, i) + side(residual, i) + side(bd, i) + orecv[i].astype(F32)).astype(BF)
     mine = pltpu.make_async_copy(theirs.at[0], outb.at[x], cs)
     mine.start()
-    away = remote(theirs.at[1], outb.at[x], ps.at[2], pr.at[2], at(1 - x, k, y))
-    away.start()
 
     exchange.wait_recv()
     g2 = xb[SEQ - 1 : PADS, :].astype(F32)[2:3]
@@ -634,7 +632,7 @@
     td, tu, to, ta, tb, rowt, colt,
     pr, sbd, rowb, colv, rr, cr, rsum, csum, rz, cz,
     ssu, rsu, lsu, sso, rso, lso, ssa, rsa, lsa, ssb, rsb, lsb, ssd, rsd,
-    lsem, zss, zrs, zls, es, er, hs, hr, cs, vs, vr, ws, wr, msem, spot, later,
+    lsem, zss, zrs, zls, es, er, hs, hr, cs, vs, vr, ws, wr, msem, spot, later, far_start,
     xb, f1b, hflat, dbr, dbrb, vec2, dbu,
     acc, gov, dqkv, do, dq,
     stu, sbu, cvu, sto, sbo, cvo, sta, sba, cva, sbb, cvb,
@@ -803,8 +801,9 @@
         mine = pltpu.make_async_copy(home.at[0], gin.at[x], cs)
         mine.start()
         away = remote(home.at[1], gin.at[x], hs, hr, at(1 - x, k, y))
+        ring_b.second()
         away.start()
-        ring_b.second()
+        far_start()
         ring_o.third()
         ring_o.fourth()
         if summed:
@@ -931,6 +930,9 @@
             + [rows4, low(full, nq), low(full, hw), low(full, ff), tall, tall],
         )
 
+        def far_start():
+            remote(r.theirs.at[1], r.outb.at[x], r.ps_m.at[2], r.pr_m.at[2], at(1 - x, k, y)).start()
+
         def later():
             far = at(1 - x, k, y)
             pltpu.make_async_copy(r.theirs.at[0], r.outb.at[x], r.cs_m).wait()
@@ -955,7 +957,7 @@
                 r.pr, r.sbd, r.rowb, r.colv, r.rr, r.cr, r.rsum, r.csum, r.rz, r.cz,
                 r.ssu, r.rsu, r.lsu, r.sso, r.rso, r.lso, r.ssa, r.rsa, r.lsa, r.ssb, r.rsb, r.lsb, r.ssd, r.rsd,
                 r.lsem_b, r.zss, r.zrs, r.zls, r.es, r.er, r.hs, r.hr, r.cs, r.vs, r.vr, r.ws, r.wr, r.msem_b,
-                spot, later, *v,
+                spot, later, far_start, *v,
             ),
             [hbm[n] for n in ("xb", "f1b", "hflat", "dbr", "dbrb", "rowv", "dbu")]
             + [wide(2, 8, full), low(full, hw), low(PADS, nq), low(4, hw, width), low(2, 4, width, nh)]

time: 365 us -> 362 us (level)
  no operation moved by 1% of the time
where the time goes in v3:
time: 362 us; the launch traced here: 359 us
  Pallas kernels  334 us (92%)
  local copies, waits for them, and re-layouts  20 us (6%)
  other arithmetic  4.65 us (1%)
    pallas_call x1, Pallas kernels, layer(): pl.pallas_call(kernel, out_shape=[jax.ShapeDtypeStruct(*v) for v in (*hbm...  334 us
    unnamed x30, local copies, waits for them, and re-layouts  8.33 us

profile of v3, /device:TPU:0, one launch (start us, length us, event | category | flops | bytes accessed | tf_op | source)
XLA Modules:
  0.0 359.2 jit_solution(11292651172343310273)
XLA Ops:
  0.6 0.7 reshape.58
  1.3 0.7 reshape.59
  2.0 0.8 fusion.4
  2.8 0.9 fusion.3
  3.7 0.7 reshape.62
  4.4 0.7 pad_add_fusion.2.refs_2_
  5.1 0.1 pad_add_fusion.1
  5.2 1.4 fusion.1
  6.5 0.3 copy.39
  6.8 0.3 copy.40
  7.1 0.0 copy-start.2
  7.1 1.3 add_add_fusion.refs_0_
  8.4 0.0 copy-done.2
  8.4 0.2 fusion
  8.6 0.3 copy.41
  8.9 0.0 copy-start
  8.9 0.3 copy.42
  9.2 1.1 pad_add_fusion.refs_1_
  10.4 0.0 copy-done
  10.4 0.3 slice_bitcast_fusion.4
  10.7 2.2 concatenate.18.refs_3_
  12.9 333.8 %layer.1 = (bf16[4,288,1792]{2,1,0:T(8,128)(2,1)}, bf16[4,288,576]{2,1,0:T(8,128)(2,1)}, bf16[4,288,2152]{2,1,0:T(8,128)(2,1)}, bf16[4,288,2152]{2,1,0:T(8,128)(...) custom-call(bf16[2,736,288]{2,1,0:T(8,128)(2,1)} %add_add_fusion.ref, ...), custom_call_target="tpu_custom_call" | custom-call | tf_op jit(solution)/shard_map/layer/pallas_call | solution.py:970
  346.6 1.3 slice_bitcast_fusion.3
  348.0 0.2 pad_maximum_fusion
  348.2 0.0 copy-start.9
  348.2 0.0 copy-start.8
  348.2 1.9 copy.36
  350.2 0.0 copy-done.9
  350.2 0.6 slice_reduce_fusion.1
  350.8 0.6 fusion.2
  351.3 0.1 slice_reduce_fusion.6
  351.4 0.6 slice_reduce_fusion
  352.1 0.1 pad_maximum_fusion.4
  352.1 0.1 pad_maximum_fusion.5
  352.2 0.6 pad_maximum_fusion.3
  352.8 0.0 copy-done.6
  352.8 0.2 reshape.63
  353.1 0.2 reshape.64
  353.4 0.0 copy-start.1
  353.4 0.3 pad_maximum_fusion.2
  353.7 0.8 copy.38
  354.5 0.1 copy-done.1
  354.6 0.1 slice_bitcast_fusion.1
  354.7 0.2 pad_maximum_fusion.1
  355.0 1.9 copy.37
  356.9 0.7 copy.46
  357.6 0.8 copy.47
  358.4 0.8 copy.48
  (13 shorter events, 0.0 us)
Async XLA Ops:
  7.1 1.3 copy-start.2
  8.9 1.4 copy-start
  348.2 2.0 copy-start.9
  348.2 3.1 copy-start.8
  348.2 4.6 %copy-start.6 = (f32[72,896]{1,0:T(8,128)S(1)}, f32[72,896]{1,0:T(8,128)}, u32[]{:S(2)}) copy-start(f32[72,896]{1,0:T(8,128)} %get-tuple-element.24) | copy-start | bytes 774148
  348.2 4.9 %copy-start.5 = (f32[72,896]{1,0:T(8,128)S(1)}, f32[72,896]{1,0:T(8,128)}, u32[]{:S(2)}) copy-start(f32[72,896]{1,0:T(8,128)} %get-tuple-element.25) | copy-start | bytes 774148
  353.4 1.3 copy-start.1
  354.9 1.9 copy-start.7
  354.9 2.6 copy-start.4
  355.0 3.4 copy-start.3
